TPU v7x, 128 devices: a whole 4x4x4 slice. The times are simulated.
128 devices in a mesh: pipe: 4 (over z_hi, core), dp: 32 (over z_lo, x, y).
Axes of the slice: x: 4, y: 4, z: 4 (z_hi: 2, z_lo: 2; z = z_hi * 2 + z_lo), core: 2. Of those that a mesh axis runs over, the one named last changes fastest.
Arguments:
- section_inputs: bfloat16 [2, 4, 128, 7168], P(None, 'pipe', None, 'dp'), may hold values from -4.5 to 4.5
- loss_grads: bfloat16 [2, 128, 7168], P(None, None, 'dp'), may hold values from -1.25 to 1.25
- live_tokens: int32 [2], replicated, may hold values from 32 to 128, as said below
- gains: bfloat16 [2, 4, 7168], P(None, 'pipe', 'dp'), as said below
- w_in: bfloat16 [2, 4, 7168, 4096], P(None, 'pipe', 'dp'), as said below
- w_out: bfloat16 [2, 4, 2048, 7168], P(None, 'pipe', None, 'dp'), as said below
- first_in: bfloat16 [4, 7168, 4096], P('pipe', 'dp'), may hold values from -6 to 6
- first_out: bfloat16 [4, 2048, 7168], P('pipe', None, 'dp'), may hold values from -6 to 6
- second_in: bfloat16 [4, 7168, 4096], P('pipe', 'dp'), may hold values from 0.049804688 to 2
- second_out: bfloat16 [4, 2048, 7168], P('pipe', None, 'dp'), may hold values from 0.049804688 to 2
Outputs:
- input_grads: bfloat16 [2, 4, 128, 7168], P(None, 'pipe', None, 'dp')
- updated_in: bfloat16 [4, 7168, 4096], P('pipe', 'dp')
- updated_out: bfloat16 [4, 2048, 7168], P('pipe', None, 'dp')
- next_first_in: bfloat16 [4, 7168, 4096], P('pipe', 'dp')
- next_first_out: bfloat16 [4, 2048, 7168], P('pipe', None, 'dp')
- next_second_in: bfloat16 [4, 7168, 4096], P('pipe', 'dp')
- next_second_out: bfloat16 [4, 2048, 7168], P('pipe', None, 'dp')
Inputs may be any that keep to these rules, and one draw needn't show every extreme that they name: `live_tokens`: rows at or beyond a chain's count are padding; one of the two counts equals 128. gains[1, p] equals gains[0, 3 - p]. w_in[1, p] equals w_in[0, 3 - p]. w_out[1, p] equals w_out[0, 3 - p].
All inputs are finite; a program needn't handle non-finite values.
Results may differ from a plain program's by a relative error of at most 0.014.
Values may be sent and summed in bfloat16 or wider, within the bound.
A program may use at most 128 MiB of HBM per device.

v0:
```python
import jax
import jax.numpy as jnp
from jax import lax
from jax.sharding import PartitionSpec as P

D = 7168


rms_eps = 1e-06
beta_first = 0.9
beta_second = 0.95
learn_rate = 0.00022
decay_rate = 0.1
adam_eps = 1e-08


def shifted(shard, axis, by):
    peers = lax.axis_size(axis)
    pairs = [(i, i + by) for i in range(peers) if 0 <= i + by < peers]
    return lax.ppermute(shard, axis, pairs)


def from_partner(shard, axis, stride):
    return lax.ppermute(shard, axis, [(i, i ^ 1 << stride) for i in range(lax.axis_size(axis))])


def pointwise(pre_sums, grad_hidden, inv_rms):
    half_width = pre_sums.shape[1] // 2
    gate_pre = pre_sums[:, :half_width]
    up_pre = pre_sums[:, half_width:]
    row_scale = inv_rms[:, None]
    gate_val = row_scale * gate_pre
    up_val = row_scale * up_pre
    sigma_gate = jax.nn.sigmoid(gate_val)
    hidden = (gate_val * sigma_gate * up_val).astype(jnp.bfloat16)
    d_gate = (
        row_scale * grad_hidden * up_val * sigma_gate * (1.0 + gate_val * (1.0 - sigma_gate))
    ).astype(jnp.bfloat16)
    d_up = (row_scale * grad_hidden * gate_val * sigma_gate).astype(jnp.bfloat16)
    both_grads = jnp.concatenate([d_gate, d_up], axis=1)
    hidden_dot = jnp.sum(
        d_gate.astype(jnp.float32) * gate_pre + d_up.astype(jnp.float32) * up_pre, axis=1
    )
    return (hidden, both_grads, hidden_dot)


def token_factor(pre_sums, grad_hidden, sum_squares):
    inv_rms = lax.rsqrt(sum_squares / D + rms_eps)
    hidden, both_grads, hidden_dot = pointwise(pre_sums, grad_hidden, inv_rms)
    return (hidden, both_grads, inv_rms)


def section_back(inputs, gain, grad_out, weight_in, weight_out):
    inputs_f = inputs.astype(jnp.float32)
    square_part = jnp.sum(inputs_f * inputs_f, axis=1)
    gained = (gain.astype(jnp.float32)[None, :] * inputs_f).astype(jnp.bfloat16)
    pre_part = jnp.dot(gained, weight_in, preferred_element_type=jnp.float32)
    grad_part = lax.dot_general(
        grad_out, weight_out, (((1,), (1,)), ((), ())), preferred_element_type=jnp.float32
    )
    pre_sums, grad_hidden, sum_squares = lax.psum((pre_part, grad_part, square_part), "dp")
    hidden, both_grads, row_factor = token_factor(pre_sums, grad_hidden, sum_squares)
    grad_gained = lax.dot_general(
        both_grads, weight_in, (((1,), (1,)), ((), ())), preferred_element_type=jnp.float32
    )
    total_dot = lax.psum(jnp.sum(grad_gained * gained.astype(jnp.float32), axis=1), "dp")
    row_coef = row_factor * row_factor * total_dot / D
    grad_in = (
        grad_out.astype(jnp.float32)
        + gain.astype(jnp.float32)[None, :] * grad_gained
        - inputs_f * row_coef[:, None]
    ).astype(jnp.bfloat16)
    return (grad_in, gained, hidden, both_grads)


def weight_terms(gained, both_grads, hidden, grad_out):
    grad_w_in = lax.dot_general(
        gained, both_grads, (((0,), (0,)), ((), ())), preferred_element_type=jnp.float32
    )
    grad_w_out = lax.dot_general(
        hidden, grad_out, (((0,), (0,)), ((), ())), preferred_element_type=jnp.float32
    )
    return (grad_w_in, grad_w_out)


def adamw(weights, first, second, grads):
    first_new = beta_first * first.astype(jnp.float32) + (1.0 - beta_first) * grads
    second_new = beta_second * second.astype(jnp.float32) + (1.0 - beta_second) * grads * grads
    weights_f = weights.astype(jnp.float32)
    weights_new = weights_f - learn_rate * (
        first_new / (jnp.sqrt(second_new) + adam_eps) + decay_rate * weights_f
    )
    return (
        weights_new.astype(jnp.bfloat16),
        first_new.astype(jnp.bfloat16),
        second_new.astype(jnp.bfloat16),
    )


def shards(
    section_inputs,
    loss_grads,
    live_tokens,
    gains,
    w_in,
    w_out,
    first_in,
    first_out,
    second_in,
    second_out,
):
    layers = lax.axis_size("pipe")
    section_index = lax.axis_index("pipe")
    inputs_local = section_inputs[:, 0]
    gains_local = gains[:, 0]
    win_local = w_in[:, 0]
    wout_local = w_out[:, 0]
    token_count = inputs_local.shape[1]
    row_ids = lax.broadcasted_iota(jnp.int32, (token_count, 1), 0)
    zero_grad = jnp.zeros(loss_grads.shape[1:], jnp.bfloat16)
    start_down = jnp.where(row_ids < live_tokens[0], loss_grads[0], zero_grad)
    start_up = jnp.where(row_ids < live_tokens[1], loss_grads[1], zero_grad)
    copy_ids = lax.broadcasted_iota(jnp.int32, (2, 1, 1), 0)
    grads_out = jnp.zeros((2,) + zero_grad.shape, jnp.bfloat16)
    accum_in = jnp.zeros((2,) + win_local.shape[1:], jnp.float32)
    accum_out = jnp.zeros((2,) + wout_local.shape[1:], jnp.float32)
    saved_gained = jnp.zeros((2,) + zero_grad.shape, jnp.bfloat16)
    saved_grads = jnp.zeros((2, token_count, win_local.shape[2]), jnp.bfloat16)
    saved_hidden = jnp.zeros((2, token_count, wout_local.shape[1]), jnp.bfloat16)
    saved_out = jnp.zeros((2,) + zero_grad.shape, jnp.bfloat16)
    recv_down = zero_grad
    recv_up = zero_grad
    for step in range(layers):
        down_active = section_index == layers - 1 - step
        up_active = section_index == step
        any_active = jnp.logical_or(down_active, up_active)
        copy_slot = jnp.where(down_active, 0, 1).astype(jnp.int32)
        if step == 0:
            grad_out = jnp.where(down_active, start_down, jnp.where(up_active, start_up, zero_grad))
        else:
            grad_out = jnp.where(down_active, recv_down, jnp.where(up_active, recv_up, zero_grad))
        inputs = lax.dynamic_index_in_dim(inputs_local, copy_slot, 0, keepdims=False)
        gain = lax.dynamic_index_in_dim(gains_local, copy_slot, 0, keepdims=False)
        weight_in = lax.dynamic_index_in_dim(win_local, copy_slot, 0, keepdims=False)
        weight_out = lax.dynamic_index_in_dim(wout_local, copy_slot, 0, keepdims=False)
        grad_in, gained, hidden, both_grads = section_back(
            inputs, gain, grad_out, weight_in, weight_out
        )
        chosen = jnp.logical_and(copy_ids == copy_slot, any_active)
        grads_out = jnp.where(chosen, grad_in[None], grads_out)
        saved_gained = jnp.where(chosen, gained[None], saved_gained)
        saved_grads = jnp.where(chosen, both_grads[None], saved_grads)
        saved_hidden = jnp.where(chosen, hidden[None], saved_hidden)
        saved_out = jnp.where(chosen, grad_out[None], saved_out)
        grad_w_in, grad_w_out = weight_terms(gained, both_grads, hidden, grad_out)
        accum_in = jnp.where(chosen, accum_in + grad_w_in[None], accum_in)
        accum_out = jnp.where(chosen, accum_out + grad_w_out[None], accum_out)
        if step < layers - 1:
            recv_down = shifted(grad_in, "pipe", -1)
            recv_up = shifted(grad_in, "pipe", 1)
    partner_grads = (accum_in[1], accum_out[1])
    for bit_index in range(layers.bit_length() - 1):
        partner_grads = from_partner((partner_grads[0], partner_grads[1]), "pipe", bit_index)
    total_in = accum_in[0] + partner_grads[0]
    total_out = accum_out[0] + partner_grads[1]
    new_in, mom_in, sec_in = adamw(win_local[0], first_in[0], second_in[0], total_in)
    new_out, mom_out, sec_out = adamw(wout_local[0], first_out[0], second_out[0], total_out)
    return (
        grads_out[:, None],
        new_in[None],
        new_out[None],
        mom_in[None],
        mom_out[None],
        sec_in[None],
        sec_out[None],
    )


def solution(mesh):
    placed = (
        P(None, "pipe", None, "dp"),
        P(None, None, "dp"),
        P(),
        P(None, "pipe", "dp"),
        P(None, "pipe", "dp", None),
        P(None, "pipe", None, "dp"),
        P("pipe", "dp", None),
        P("pipe", None, "dp"),
        P("pipe", "dp", None),
        P("pipe", None, "dp"),
    )
    return jax.shard_map(
        shards,
        mesh=mesh,
        in_specs=placed,
        out_specs=(
            P(None, "pipe", None, "dp"),
            P("pipe", "dp", None),
            P("pipe", None, "dp"),
            P("pipe", "dp", None),
            P("pipe", None, "dp"),
            P("pipe", "dp", None),
            P("pipe", None, "dp"),
        ),
        check_vma=False,
    )
```

profile of v0, /device:TPU:0, one launch (start us, length us, event | category | flops | bytes accessed | tf_op | source)
XLA Modules:
  0.0 1738.8 jit_solution(2968394377446355591)
XLA Ops:
  7.3 1.4 fusion.164
  8.6 1.3 iota_compare_fusion
  9.9 0.8 fusion.149
  10.8 3.4 fusion.28
  14.2 1.3 fusion.49
  15.7 83.5 %psum.112 = f32[128]{0:T(128)S(1)} all-reduce(f32[128]{0:T(128)S(1)} %fusion.76), channel_id=1, replica_groups=mesh['pipe'=4,'dp'=32] {'dp'}, use_global_device_ids=true, to_apply=%region_1.2 | all-reduce | flops 128 | bytes 1024 | tf_op jit(solution)/shard_map/psum | solution.py:61
  99.2 237.5 %all-reduce.18.cloned.1.call-done = (f32[128,2048]{1,0:T(8,128)}, f32[128,4096]{1,0:T(8,128)}) async-done(((f32[128,2048]{1,0:T(8,128)}, f32[128,4096]{1,0:T(8,128)}), (f32[128,2048]{1,0:T(8,128)}, f32[128,4096]{1,0:T(8,128)})) %all-reduce.18.cloned.1.call-update) | async-done | bytes 3145744 | tf_op jit(solution)/shard_map/psum | solution.py:61
  336.7 2.6 multiply_convert_fusion.11
  339.4 0.4 copy-done.1
  339.7 1.1 fusion.91
  340.8 82.2 %all-reduce.2 = (f32[128]{0:T(128)S(1)}, f32[128]{0:T(128)S(1)}) all-reduce(f32[128]{0:T(128)S(1)} %get-tuple-element.8, f32[128]{0:T(128)S(1)} %get-tuple-element.9), channel_id=1, replica_groups=mesh['pipe'=4,'dp'=32] {'dp'}, use_global_device_ids=true, to_apply=%region_5.6 | all-reduce | flops 256 | bytes 2048 | tf_op jit(solution)/shard_map/psum | solution.py:66
  423.1 1.3 collective-permute-start.1
  424.4 1.3 collective-permute-start
  425.7 3.4 fusion.24
  429.1 1.5 collective-permute-done
  430.6 1.3 fusion.47
  432.0 317.5 %all-reduce.16.cloned.1.call-done = (f32[128,2048]{1,0:T(8,128)}, f32[128,4096]{1,0:T(8,128)}) async-done(((f32[128,2048]{1,0:T(8,128)}, f32[128,4096]{1,0:T(8,128)}), (f32[128,2048]{1,0:T(8,128)}, f32[128,4096]{1,0:T(8,128)})) %all-reduce.16.cloned.1.call-update) | async-done | bytes 3145744 | tf_op jit(solution)/shard_map/psum | solution.py:61
  749.5 2.6 multiply_convert_fusion.9
  752.2 0.3 copy-done.2
  752.5 0.6 multiply_reduce_fusion.2
  753.2 82.3 %all-reduce.1 = (f32[128]{0:T(128)S(1)}, f32[128]{0:T(128)S(1)}) all-reduce(f32[128]{0:T(128)S(1)} %get-tuple-element.46, f32[128]{0:T(128)S(1)} %get-tuple-element.10), channel_id=1, replica_groups=mesh['pipe'=4,'dp'=32] {'dp'}, use_global_device_ids=true, to_apply=%region_11.12 | all-reduce | flops 256 | bytes 2048 | tf_op jit(solution)/shard_map/psum | solution.py:66
  835.6 1.3 collective-permute-start.3
  836.9 1.3 collective-permute-start.2
  838.2 3.4 fusion.20
  841.6 1.5 collective-permute-done.2
  843.1 1.3 fusion.45
  844.5 317.7 %all-reduce.14.cloned.1.call-done = (f32[128,2048]{1,0:T(8,128)}, f32[128,4096]{1,0:T(8,128)}) async-done(((f32[128,2048]{1,0:T(8,128)}, f32[128,4096]{1,0:T(8,128)}), (f32[128,2048]{1,0:T(8,128)}, f32[128,4096]{1,0:T(8,128)})) %all-reduce.14.cloned.1.call-update) | async-done | bytes 3145744 | tf_op jit(solution)/shard_map/psum | solution.py:61
  1162.2 2.6 multiply_convert_fusion.7
  1165.2 1.3 multiply_reduce_fusion.1
  1166.5 82.2 %all-reduce = (f32[128]{0:T(128)S(1)}, f32[128]{0:T(128)S(1)}) all-reduce(f32[128]{0:T(128)S(1)} %get-tuple-element.48, f32[128]{0:T(128)S(1)} %copy-done.29), channel_id=1, replica_groups=mesh['pipe'=4,'dp'=32] {'dp'}, use_global_device_ids=true, to_apply=%region_17.18 | all-reduce | flops 256 | bytes 2048 | tf_op jit(solution)/shard_map/psum | solution.py:66
  1248.7 1.0 fusion.89
  1249.7 1.3 collective-permute-start.5
  1251.0 1.3 collective-permute-start.4
  1252.3 3.4 fusion.16
  1255.7 1.5 collective-permute-done.4
  1257.2 1.3 fusion.43
  1258.6 2.5 fusion.59
  1261.1 2.6 fusion.58
  1263.7 2.5 fusion.57
  1266.2 309.9 %all-reduce.12.cloned.1.call-done = (f32[128,2048]{1,0:T(8,128)}, f32[128,4096]{1,0:T(8,128)}) async-done(((f32[128,2048]{1,0:T(8,128)}, f32[128,4096]{1,0:T(8,128)}), (f32[128,2048]{1,0:T(8,128)}, f32[128,4096]{1,0:T(8,128)})) %all-reduce.12.cloned.1.call-update) | async-done | bytes 3145744 | tf_op jit(solution)/shard_map/psum | solution.py:61
  1576.1 2.6 multiply_convert_fusion.5
  1578.7 0.7 fusion.56
  1579.6 1.6 copy-done.7
  1581.2 3.7 add_select_fusion
  1585.0 0.4 slice_bitcast_fusion
  1585.4 2.8 copy-done
  1588.2 0.6 fusion.60
  1588.7 1.0 copy-done.12
  1589.7 0.6 fusion.61
  1590.4 1.0 copy-done.13
  1591.3 0.6 fusion.62
  1592.0 1.0 copy-done.14
  1592.9 0.6 fusion.63
  1593.6 1.3 add_select_fusion.3
  1595.2 3.0 collective-permute-start.7
  1598.1 0.9 collective-permute-done.8
  1599.1 2.9 collective-permute-start.9
  1602.0 1.3 multiply_reduce_fusion
  1603.3 83.1 %psum.127 = f32[128]{0:T(128)S(1)} all-reduce(f32[128]{0:T(128)S(1)} %get-tuple-element.50), channel_id=1, replica_groups=mesh['pipe'=4,'dp'=32] {'dp'}, use_global_device_ids=true, to_apply=%region_23.24 | all-reduce | flops 128 | bytes 1024 | tf_op jit(solution)/shard_map/psum | solution.py:66
  1686.4 1.1 fusion.94
  1687.5 0.7 select_select_fusion
  1688.3 31.2 %collective-permute-done.9 = f32[2048,224]{0,1:T(8,128)} collective-permute-done((f32[2048,224]{0,1:T(8,128)}, f32[2048,224]{0,1:T(8,128)}, u32[]{:S(2)}, u32[]{:S(2)}) %collective-permute-start.9) | collective-permute-done | bytes 1835040 | tf_op jit(solution)/shard_map/ppermute | solution.py:24
  1719.4 6.0 fusion.41
  1725.5 6.8 fusion.7
  (90 shorter events, 1.6 us)
Async XLA Ops:
  7.2 7.1 copy-start.9
  7.2 7.0 copy-start.28
  7.2 329.5 %all-reduce.18.cloned.1.call-start = ((), (), s32[]{:S(2)}) async-start(), calls=%async_computation.3 | async-start | bytes 6291456 | tf_op jit(solution)/shard_map/psum | solution.py:61
  14.2 1.4 copy-start.10
  15.6 733.9 %all-reduce.16.cloned.1.call-start = ((), (), s32[]{:S(2)}) async-start(), calls=%async_computation.2 | async-start | bytes 6291456 | tf_op jit(solution)/shard_map/psum | solution.py:61
  336.7 3.0 copy-start.1
  423.1 6.0 collective-permute-start.1
  424.4 6.2 collective-permute-start
  431.9 730.2 %all-reduce.14.cloned.1.call-start = ((), (), s32[]{:S(2)}) async-start(), calls=%async_computation.1 | async-start | bytes 6291456 | tf_op jit(solution)/shard_map/psum | solution.py:61
  749.5 3.0 copy-start.2
  752.1 1.0 copy-start.15
  752.2 1.0 copy-start.17
  835.6 6.0 collective-permute-start.3
  836.9 6.2 collective-permute-start.2
  844.4 731.6 %all-reduce.12.cloned.1.call-start = ((), (), s32[]{:S(2)}) async-start(), calls=%async_computation | async-start | bytes 6291456 | tf_op jit(solution)/shard_map/psum | solution.py:61
  1162.2 3.0 copy-start.3
  1164.8 1.6 copy-start.19
  1164.8 1.6 copy-start.21
  1164.8 1.6 copy-start.29
  1249.7 6.0 collective-permute-start.5
  1251.0 6.2 collective-permute-start.4
  1258.6 2.5 copy-start.16
  1258.6 2.5 copy-start.18
  1261.1 2.6 copy-start.20
  1261.1 2.6 copy-start.22
  1576.0 3.6 copy-start.8
  1578.7 0.8 copy-start.23
  1578.7 1.0 copy-start.25
  1578.7 2.5 copy-start.7
  1584.9 3.2 copy-start
  1585.0 3.2 copy-start.11
  1588.1 1.6 copy-start.12
  1588.1 7.0 collective-permute-start.6
  1589.7 1.6 copy-start.13
  1591.3 1.6 copy-start.14
  1593.5 8.4 copy-start.24
  1593.6 8.4 copy-start.26
  1594.8 8.4 copy-start.6
  1594.9 7.1 copy-start.4
  1595.1 4.0 collective-permute-start.8
  1595.2 130.3 %collective-permute-start.7 = (f32[224,4096]{1,0:T(8,128)}, f32[224,4096]{1,0:T(8,128)}, u32[]{:S(2)}, u32[]{:S(2)}) collective-permute-start(f32[224,4096]{1,0:T(8,128)} %collective-permute-done.6), channel_id=1, source_target_pairs={{0,64},{32,96},{64,0},{96,32},{1,65},{33,97},{65,1},{97,33},{2,66}... | collective-permute-start | bytes 11010056 | tf_op jit(solution)/shard_map/ppermute | solution.py:24
  1599.1 120.4 %collective-permute-start.9 = (f32[2048,224]{0,1:T(8,128)}, f32[2048,224]{0,1:T(8,128)}, u32[]{:S(2)}, u32[]{:S(2)}) collective-permute-start(f32[2048,224]{0,1:T(8,128)} %collective-permute-done.8), channel_id=1, source_target_pairs={{0,64},{32,96},{64,0},{96,32},{1,65},{33,97},{65,1},{97,33},{2,66}... | collective-permute-start | bytes 5505032 | tf_op jit(solution)/shard_map/ppermute | solution.py:24
  1602.0 123.5 %slice-start = ((s8[7340032]{0:T(1024)(128)(4,1)}), s8[3145728]{0:T(1024)(128)(4,1)S(1)}, s32[]{:S(2)}) async-start(s8[7340032]{0:T(1024)(128)(4,1)} %bitcast.245), calls=%async_computation.4 | async-start | bytes 6291456
  1686.4 39.0 %copy-start.27 = (bf16[1,224,4096]{2,1,0:T(8,128)(2,1)S(1)}, bf16[1,224,4096]{2,1,0:T(8,128)(2,1)}, u32[]{:S(2)}) copy-start(bf16[1,224,4096]{2,1,0:T(8,128)(2,1)} %param.18) | copy-start | bytes 5505028
  1688.3 37.2 %slice-start.1 = ((s8[7340032]{0:T(1024)(128)(4,1)}), s8[4194304]{0:T(1024)(128)(4,1)S(1)}, s32[]{:S(2)}) async-start(s8[7340032]{0:T(1024)(128)(4,1)} %bitcast.245), calls=%async_computation.5 | async-start | bytes 8388608
  1688.3 37.2 %copy-start.5 = (bf16[2,1,224,4096]{3,2,1,0:T(8,128)(2,1)S(1)}, bf16[2,1,224,4096]{3,2,1,0:T(8,128)(2,1)}, u32[]{:S(2)}) copy-start(bf16[2,1,224,4096]{3,2,1,0:T(8,128)(2,1)} %param.14) | copy-start | bytes 11010052
Sparse Core Ops, SparseCore 0:
  15.7 320.9 all-reduce.17
  432.1 317.4 all-reduce.15
  844.6 317.5 all-reduce.13
  1258.7 317.3 all-reduce.11
where the time goes:
time: 1740 us
  waiting for transfers between devices  1220 us (70%)
  blocking collectives  413 us (24%)
  matrix products  33.9 us (2%)
  other arithmetic  33.6 us (2%)
    psum x4, waiting for transfers between devices, section_back(): lax.psum((pre_part, grad_part, square_part), 'dp')  1180 us
    psum x4, blocking collectives, section_back(): lax.psum(jnp.sum(grad_gained * gained.astype(jnp.float32), axis=1), 'dp')  330 us
    psum x1, blocking collectives, section_back(): lax.psum((pre_part, grad_part, square_part), 'dp')  83.5 us
  transfers between devices with their start and end apart: 14, of which 9 were waited for; matrix products, arithmetic and copies ran while one was open for 2% of the time, Pallas kernels for 0%

commit v1 on v0

v1 whole, which is shorter than its diff:
```python
import functools

import jax
import jax.numpy as jnp
from jax import lax
from jax.experimental import pallas as pl
from jax.experimental.pallas import tpu as pltpu
from jax.sharding import PartitionSpec as P

rms_eps = 1e-06
beta_first = 0.9
beta_second = 0.95
learn_rate = 0.00022
decay_rate = 0.1
adam_eps = 1e-08

BF16 = jnp.bfloat16
F32 = jnp.float32
LANES = 128

PRE_SUM, PRE_ALL, GRAD_SUM, GRAD_ALL, HAND = 0, 2, 4, 6, 8
STATS, MIR_GAINED, MIR_OUT, MIR_PRE, MIR_GRAD, MIR_RMS = 10, 11, 12, 13, 14, 15


def dot_nt(left, right):
    return lax.dot_general(left, right, (((1,), (1,)), ((), ())), preferred_element_type=F32)


def dot_tn(left, right):
    return lax.dot_general(left, right, (((0,), (0,)), ((), ())), preferred_element_type=F32)


def await_bytes(ref, sem):
    pltpu.make_async_copy(ref, ref, sem).wait()


def relay_kernel(
    n,
    live_ref,
    x_ref,
    loss_ref,
    gain_ref,
    win_ref,
    wout_ref,
    both_ref,
    hid_ref,
    gained_ref,
    gout_ref,
    gin_ref,
    gained_s,
    pre_send,
    pre_recv,
    pre_full,
    grad_send,
    grad_recv,
    grad_full,
    stat_all,
    rms_s,
    gate_coef,
    up_coef,
    dot_coef,
    hand,
    next_s,
    gained_mir,
    out_mir,
    send_sems,
    recv_sems,
):
    pipe = lax.axis_index("pipe")
    me = lax.axis_index("dp")
    high = pipe // 2
    inner = (pipe * (3 - pipe)) // 2
    section = (1 - high, high)
    half = n // 2
    tokens = x_ref.shape[2]
    rows = tokens // 2
    hidden = wout_ref.shape[2]
    width = n * x_ref.shape[3]
    chunks = hidden // 256
    across = lax.rem(me + half, n)

    barrier = pltpu.get_barrier_semaphore()

    def greet(step, carry):
        pl.semaphore_signal(barrier, inc=1, device_id={"dp": lax.rem(me + step, n)})
        return carry

    lax.fori_loop(1, n, greet, 0)
    for step in range(1, 4):
        pl.semaphore_signal(barrier, inc=1, device_id={"pipe": lax.rem(pipe + step, 4)})
    pl.semaphore_signal(barrier, inc=1, device_id={"pipe": 3 - pipe, "dp": across})

    def spread(source, target, slot):
        def one(step, carry):
            peer = lax.rem(me + step, n)
            pltpu.make_async_remote_copy(
                src_ref=source(peer),
                dst_ref=target,
                send_sem=send_sems.at[slot],
                recv_sem=recv_sems.at[slot],
                device_id={"dp": peer},
            ).start()
            return carry

        lax.fori_loop(1, n, one, 0)

    def remote(source, target, slot, where):
        pltpu.make_async_remote_copy(
            src_ref=source,
            dst_ref=target,
            send_sem=send_sems.at[slot],
            recv_sem=recv_sems.at[slot],
            device_id=where,
        ).start()

    def pre_partial(k):
        inputs_f = x_ref[section[k], 0].astype(F32)
        gained = (gain_ref[section[k]].astype(F32) * inputs_f).astype(BF16)
        gained_s[k] = gained
        ones = jnp.ones((8, inputs_f.shape[1]), F32)
        stat_all[me, pl.ds(8 * k, 8), :] = lax.dot_general(
            ones,
            inputs_f * inputs_f,
            (((1,), (1,)), ((), ())),
            preferred_element_type=F32,
            precision=lax.Precision.HIGHEST,
        )

        def chunk(c, carry):
            for part in range(2):
                columns = pl.ds(pl.multiple_of(part * hidden + c * 256, 256), 256)
                sums = jnp.dot(
                    gained, win_ref[section[k], 0, :, columns], preferred_element_type=F32
                ).astype(BF16)
                for q in range(2):
                    for th in range(2):
                        pre_send[k, th * half + 2 * c + q, part] = sums[
                            th * rows : (th + 1) * rows, q * LANES : (q + 1) * LANES
                        ]
            return carry

        lax.fori_loop(0, chunks, chunk, 0)
        pre_recv[k, me] = pre_send[k, me]

    def pre_reduce(k):
        await_bytes(pre_recv.at[k, pl.ds(0, n - 1)], recv_sems.at[PRE_SUM + k])
        for part in range(2):
            total = lax.fori_loop(
                0,
                n,
                lambda j, acc: acc + pre_recv[k, j, part].astype(F32),
                jnp.zeros((rows, LANES), F32),
            )
            pre_full[k, me, part] = total.astype(BF16)
        spread(lambda peer: pre_full.at[k, me], pre_full.at[k, me], PRE_ALL + k)

    def coefficients(k, row_at):
        for th in range(2):
            scale = rms_s[k, pl.ds(th * rows, rows), :]

            def block(fb, carry):
                j = th * half + fb
                gate_pre = pre_full[k, j, 0].astype(F32)
                up_pre = pre_full[k, j, 1].astype(F32)
                gate_val = scale * gate_pre
                up_val = scale * up_pre
                sigma = jax.nn.sigmoid(gate_val)
                swish = gate_val * sigma
                for_gate = scale * up_val * sigma * (1.0 + gate_val * (1.0 - sigma))
                for_up = scale * swish
                gate_coef[k, j] = for_gate
                up_coef[k, j] = for_up
                dot_coef[k, j] = for_gate * gate_pre + for_up * up_pre
                hid_ref[
                    pl.ds(row_at + th * rows, rows), pl.ds(pl.multiple_of(fb * LANES, LANES), LANES)
                ] = (swish * up_val).astype(BF16)
                return carry

            lax.fori_loop(0, half, block, 0)

    def both_grads(k, row_at):
        dots = []
        for th in range(2):

            def block(fb, acc):
                j = th * half + fb
                grad_hidden = grad_full[k, j].astype(F32)
                at = pl.ds(row_at + th * rows, rows)
                both_ref[at, pl.ds(pl.multiple_of(fb * LANES, LANES), LANES)] = (
                    grad_hidden * gate_coef[k, j]
                ).astype(BF16)
                both_ref[at, pl.ds(pl.multiple_of(hidden + fb * LANES, LANES), LANES)] = (
                    grad_hidden * up_coef[k, j]
                ).astype(BF16)
                return acc + grad_hidden * dot_coef[k, j]

            acc = lax.fori_loop(0, half, block, jnp.zeros((rows, LANES), F32))
            dots.append(jnp.sum(acc, axis=1, keepdims=True))
        return jnp.concatenate(dots, axis=0)

    def chain(k):
        sec = section[k]
        grad_out = hand[k]

        def chunk(c, carry):
            weights = wout_ref[sec, 0, pl.ds(pl.multiple_of(c * 256, 256), 256), :]
            sums = dot_nt(grad_out, weights).astype(BF16)
            for q in range(2):
                for th in range(2):
                    grad_send[k, th * half + 2 * c + q] = sums[
                        th * rows : (th + 1) * rows, q * LANES : (q + 1) * LANES
                    ]
            return carry

        lax.fori_loop(0, chunks, chunk, 0)
        grad_recv[k, me] = grad_send[k, me]
        spread(lambda peer: grad_send.at[k, peer], grad_recv.at[k, me], GRAD_SUM + k)
        await_bytes(grad_recv.at[k, pl.ds(0, n - 1)], recv_sems.at[GRAD_SUM + k])
        total = lax.fori_loop(
            0,
            n,
            lambda j, acc: acc + grad_recv[k, j].astype(F32),
            jnp.zeros((rows, LANES), F32),
        )
        grad_full[k, me] = total.astype(BF16)
        spread(lambda peer: grad_full.at[k, me], grad_full.at[k, me], GRAD_ALL + k)
        await_bytes(grad_full.at[k, pl.ds(0, n - 1)], recv_sems.at[GRAD_ALL + k])

        @pl.when(sec == 1)
        def _():
            remote(grad_full.at[k], grad_full.at[2], MIR_GRAD, {"pipe": 3 - pipe, "dp": across})
            remote(hand.at[k], out_mir, MIR_OUT, {"pipe": 3 - pipe})

        row_at = pl.multiple_of(sec * tokens, tokens)
        hidden_dot = both_grads(k, row_at)

        def part(c, acc):
            columns = pl.ds(pl.multiple_of(c * 512, 512), 512)
            return acc + dot_nt(both_ref[pl.ds(row_at, tokens), columns], win_ref[sec, 0, :, columns])

        grad_gained = lax.fori_loop(
            0, 2 * hidden // 512, part, jnp.zeros((tokens, x_ref.shape[3]), F32)
        )
        inv_rms = rms_s[k, :, 0:1]
        row_coef = inv_rms * inv_rms * hidden_dot / width
        grad_in = (
            grad_out.astype(F32)
            + gain_ref[sec].astype(F32) * grad_gained
            - x_ref[sec, 0].astype(F32) * row_coef
        ).astype(BF16)
        gin_ref[sec, 0] = grad_in
        next_s[k] = grad_in

    pre_partial(0)
    pl.semaphore_wait(barrier, n + 3)
    spread(lambda peer: pre_send.at[0, peer], pre_recv.at[0, me], PRE_SUM)
    pre_partial(1)
    spread(lambda peer: stat_all.at[me], stat_all.at[me], STATS)
    spread(lambda peer: pre_send.at[1, peer], pre_recv.at[1, me], PRE_SUM + 1)
    remote(gained_s.at[high], gained_mir, MIR_GAINED, {"pipe": 3 - pipe})

    @pl.when(inner == 0)
    def _():
        row_ids = lax.broadcasted_iota(jnp.int32, (tokens, loss_ref.shape[2]), 0)
        start = loss_ref[section[0]]
        live = jnp.where(section[0] == 0, live_ref[0], live_ref[1])
        hand[0] = jnp.where(row_ids < live, start, jnp.zeros_like(start))

    pre_reduce(0)
    await_bytes(stat_all.at[pl.ds(0, n - 1)], recv_sems.at[STATS])
    for k in range(2):
        stats = lax.fori_loop(
            0,
            n,
            lambda j, acc: acc + stat_all[j, pl.ds(8 * k, 8), :],
            jnp.zeros((8, tokens), F32),
        )
        eighth = jnp.full((8, LANES), 0.125, F32)
        sum_squares = lax.dot_general(
            stats,
            eighth,
            (((0,), (0,)), ((), ())),
            preferred_element_type=F32,
            precision=lax.Precision.HIGHEST,
        )
        rms_s[k] = lax.rsqrt(sum_squares / width + rms_eps)
    remote(rms_s.at[high], rms_s.at[2], MIR_RMS, {"pipe": 3 - pipe, "dp": across})
    pre_reduce(1)
    for k in range(2):
        await_bytes(pre_full.at[k, pl.ds(0, n - 1)], recv_sems.at[PRE_ALL + k])
        coefficients(k, pl.multiple_of(section[k] * tokens, tokens))
    remote(pre_full.at[high], pre_full.at[2], MIR_PRE, {"pipe": 3 - pipe, "dp": across})

    @pl.when(inner == 1)
    def _():
        await_bytes(hand.at[0], recv_sems.at[HAND])

    chain(0)
    pltpu.make_async_remote_copy(
        src_ref=next_s.at[0],
        dst_ref=hand.at[inner],
        send_sem=send_sems.at[HAND],
        recv_sem=recv_sems.at[HAND + inner],
        device_id={"pipe": pipe + 1 - 2 * high},
    ).start()
    await_bytes(hand.at[1], recv_sems.at[HAND + 1])
    chain(1)

    @pl.when(inner == 1)
    def _():
        remote(next_s.at[1], hand.at[1], HAND + 1, {"pipe": pipe - 1 + 2 * high})

    await_bytes(rms_s.at[2], recv_sems.at[MIR_RMS])
    await_bytes(pre_full.at[2], recv_sems.at[MIR_PRE])
    coefficients(2, tokens)
    await_bytes(grad_full.at[2], recv_sems.at[MIR_GRAD])
    both_grads(2, tokens)
    await_bytes(gained_mir, recv_sems.at[MIR_GAINED])
    await_bytes(out_mir, recv_sems.at[MIR_OUT])
    gained_ref[pl.ds(0, tokens)] = gained_s[1 - high]
    gained_ref[pl.ds(tokens, tokens)] = gained_mir[...]
    gout_ref[pl.ds(0, tokens)] = hand[1 - high]
    gout_ref[pl.ds(tokens, tokens)] = out_mir[...]

    for k in range(2):
        await_bytes(pre_send.at[k, pl.ds(0, n - 1)], send_sems.at[PRE_SUM + k])
        await_bytes(pre_full.at[k, pl.ds(0, n - 1)], send_sems.at[PRE_ALL + k])
        await_bytes(grad_send.at[k, pl.ds(0, n - 1)], send_sems.at[GRAD_SUM + k])
        await_bytes(grad_full.at[k, pl.ds(0, n - 1)], send_sems.at[GRAD_ALL + k])
    await_bytes(stat_all.at[pl.ds(0, n - 1)], send_sems.at[STATS])
    await_bytes(gained_mir, send_sems.at[MIR_GAINED])
    await_bytes(out_mir, send_sems.at[MIR_OUT])
    await_bytes(pre_full.at[2], send_sems.at[MIR_PRE])
    await_bytes(grad_full.at[2], send_sems.at[MIR_GRAD])
    await_bytes(rms_s.at[2], send_sems.at[MIR_RMS])
    await_bytes(next_s.at[0], send_sems.at[HAND])

    @pl.when(inner == 1)
    def _():
        await_bytes(next_s.at[1], send_sems.at[HAND + 1])


def adamw(weights, first, second, grads):
    first_new = beta_first * first.astype(F32) + (1.0 - beta_first) * grads
    second_new = beta_second * second.astype(F32) + (1.0 - beta_second) * grads * grads
    weights_f = weights.astype(F32)
    weights_new = weights_f - learn_rate * (
        first_new / (jnp.sqrt(second_new) + adam_eps) + decay_rate * weights_f
    )
    return (weights_new.astype(BF16), first_new.astype(BF16), second_new.astype(BF16))


def update_kernel(
    both_ref,
    hid_ref,
    gained_ref,
    gout_ref,
    win_ref,
    wout_ref,
    fin_ref,
    fout_ref,
    sin_ref,
    sout_ref,
    nwin_ref,
    nwout_ref,
    nfin_ref,
    nfout_ref,
    nsin_ref,
    nsout_ref,
):
    grad_in = dot_tn(gained_ref[...], both_ref[...])
    nwin_ref[0], nfin_ref[0], nsin_ref[0] = adamw(
        win_ref[0, 0], fin_ref[0], sin_ref[0], grad_in
    )
    grad_out = dot_tn(hid_ref[...], gout_ref[...])
    nwout_ref[0], nfout_ref[0], nsout_ref[0] = adamw(
        wout_ref[0, 0], fout_ref[0], sout_ref[0], grad_out
    )


def shards(
    section_inputs,
    loss_grads,
    live_tokens,
    gains,
    w_in,
    w_out,
    first_in,
    first_out,
    second_in,
    second_out,
):
    n = lax.axis_size("dp")
    tokens, local = section_inputs.shape[2:]
    hidden = w_out.shape[2]
    rows = tokens // 2
    vmem = pl.BlockSpec(memory_space=pltpu.VMEM)
    blocks = (n, rows, LANES)
    both, hid, gained, gout, gin = pl.pallas_call(
        functools.partial(relay_kernel, n),
        out_shape=(
            jax.ShapeDtypeStruct((2 * tokens, 2 * hidden), BF16),
            jax.ShapeDtypeStruct((2 * tokens, hidden), BF16),
            jax.ShapeDtypeStruct((2 * tokens, local), BF16),
            jax.ShapeDtypeStruct((2 * tokens, local), BF16),
            jax.ShapeDtypeStruct(section_inputs.shape, BF16),
        ),
        in_specs=[pl.BlockSpec(memory_space=pltpu.SMEM)] + [vmem] * 5,
        out_specs=(vmem,) * 5,
        scratch_shapes=[
            pltpu.VMEM((2, tokens, local), BF16),
            pltpu.VMEM((2, n, 2, rows, LANES), BF16),
            pltpu.VMEM((2, n, 2, rows, LANES), BF16),
            pltpu.VMEM((3, n, 2, rows, LANES), BF16),
            pltpu.VMEM((2,) + blocks, BF16),
            pltpu.VMEM((2,) + blocks, BF16),
            pltpu.VMEM((3,) + blocks, BF16),
            pltpu.VMEM((n, 16, tokens), F32),
            pltpu.VMEM((3, tokens, LANES), F32),
            pltpu.VMEM((3,) + blocks, F32),
            pltpu.VMEM((3,) + blocks, F32),
            pltpu.VMEM((3,) + blocks, F32),
            pltpu.VMEM((2, tokens, local), BF16),
            pltpu.VMEM((2, tokens, local), BF16),
            pltpu.VMEM((tokens, local), BF16),
            pltpu.VMEM((tokens, local), BF16),
            pltpu.SemaphoreType.DMA((16,)),
            pltpu.SemaphoreType.DMA((16,)),
        ],
        compiler_params=pltpu.CompilerParams(
            collective_id=0, has_side_effects=True, vmem_limit_bytes=60 * 1024 * 1024
        ),
        name="relay",
    )(live_tokens, section_inputs, loss_grads, gains, w_in, w_out)

    steps = 8
    wide, tall = 2 * hidden // steps, hidden // steps
    in_block = pl.BlockSpec((1, local, wide), lambda i: (0, 0, i))
    out_block = pl.BlockSpec((1, tall, local), lambda i: (0, i, 0))
    whole = pl.BlockSpec((2 * tokens, local), lambda i: (0, 0))
    new_in, new_out, mom_in, mom_out, sec_in, sec_out = pl.pallas_call(
        update_kernel,
        grid=(steps,),
        out_shape=tuple(
            jax.ShapeDtypeStruct(a.shape, BF16)
            for a in (first_in, first_out, first_in, first_out, second_in, second_out)
        ),
        in_specs=[
            pl.BlockSpec((2 * tokens, wide), lambda i: (0, i)),
            pl.BlockSpec((2 * tokens, tall), lambda i: (0, i)),
            whole,
            whole,
            pl.BlockSpec((1, 1, local, wide), lambda i: (0, 0, 0, i)),
            pl.BlockSpec((1, 1, tall, local), lambda i: (0, 0, i, 0)),
            in_block,
            out_block,
            in_block,
            out_block,
        ],
        out_specs=(in_block, out_block) * 3,
        compiler_params=pltpu.CompilerParams(vmem_limit_bytes=60 * 1024 * 1024),
        name="update",
    )(both, hid, gained, gout, w_in, w_out, first_in, first_out, second_in, second_out)
    return (gin, new_in, new_out, mom_in, mom_out, sec_in, sec_out)


def solution(mesh):
    placed = (
        P(None, "pipe", None, "dp"),
        P(None, None, "dp"),
        P(),
        P(None, "pipe", "dp"),
        P(None, "pipe", "dp", None),
        P(None, "pipe", None, "dp"),
        P("pipe", "dp", None),
        P("pipe", None, "dp"),
        P("pipe", "dp", None),
        P("pipe", None, "dp"),
    )
    return jax.shard_map(
        shards,
        mesh=mesh,
        in_specs=placed,
        out_specs=(
            P(None, "pipe", None, "dp"),
            P("pipe", "dp", None),
            P("pipe", None, "dp"),
            P("pipe", "dp", None),
            P("pipe", None, "dp"),
            P("pipe", "dp", None),
            P("pipe", None, "dp"),
        ),
        check_vma=False,
    )
```

time: 1740 us -> 196 us (0.11)
  waiting for transfers between devices: 1220 us -> 0 us
  blocking collectives: 413 us -> 0 us
  Pallas kernels: 0 us -> 178 us
  matrix products: 33.9 us -> 0 us
  other arithmetic: 33.6 us -> 0 us
    psum x4 -> x0, waiting for transfers between devices: 1180 us -> none  [section_back(): lax.psum((pre_part, grad_part, square_part), 'dp')]
    psum x5 -> x0, blocking collectives: 413 us -> none  [the longest x4 330 us: section_back(): lax.psum(jnp.sum(grad_gained * gained.astype(jnp.float32), axis=1), 'dp')]
    pallas_call x0 -> x2, Pallas kernels: none -> 178 us  [the longest x1 165 us: shards(): pl.pallas_call(functools.partial(relay_kernel, n), out_shape=(jax.ShapeDt...]
    ppermute x10 -> x0, waiting for transfers between devices: 36.6 us -> none  [the longest x4 32.1 us: from_partner(): lax.ppermute(shard, axis, [(i, i ^ 1 << stride) for i in range(lax.axis_s...]
    dot_general x20 -> x0, matrix products: 33.9 us -> none  [the longest x4 13.7 us: section_back(): pre_part = jnp.dot(gained, weight_in, preferred_element_type=jnp.float32)]
  transfers between devices with their start and end apart: 14 -> 0, of which waited for: 9 -> 0; matrix products, arithmetic and copies ran while one was open for 2% -> 0% of each run, Pallas kernels for 0% -> 0%
where the time goes in v1:
time: 196 us
  Pallas kernels  178 us (91%)
  local copies, waits for them, and re-layouts  17.3 us (9%)
    pallas_call x1, Pallas kernels, shards(): pl.pallas_call(functools.partial(relay_kernel, n), out_shape=(jax.ShapeDt...  165 us
    unnamed x18, local copies, waits for them, and re-layouts  17.3 us
    pallas_call x1, Pallas kernels, shards(): pl.pallas_call(update_kernel, grid=(steps,), out_shape=tuple((jax.ShapeDt...  12.5 us

profile of v1, /device:TPU:0, one launch (start us, length us, event | category | flops | bytes accessed | tf_op | source)
XLA Modules:
  0.0 195.6 jit_solution(785281642530583821)
XLA Ops:
  0.6 0.0 copy-start.3
  0.6 1.3 copy.19.gain_ref
  2.0 1.7 copy.17.x_ref
  3.6 1.7 copy.18.loss_ref
  5.3 0.0 copy-start
  5.3 2.4 %copy.22.fout_ref = bf16[1,2048,224]{2,1,0:T(8,128)(2,1)} copy(bf16[1,2048,224]{1,2,0:T(8,128)(2,1)} %param.17) | data formatting | bytes 1835008 | tf_op args[7]
  7.7 0.0 copy-done.3
  7.7 1.3 copy.23.sout_ref
  9.0 0.0 copy-done
  9.0 2.4 %copy.20.wout_ref = bf16[2,1,2048,224]{3,2,1,0:T(8,128)(2,1)} copy(bf16[2,1,2048,224]{2,3,1,0:T(8,128)(2,1)S(1)} %copy-done) | data formatting | bytes 3670016 | tf_op args[5]
  11.4 165.2 %relay.1 = (bf16[256,4096]{1,0:T(8,128)(2,1)}, bf16[256,2048]{1,0:T(8,128)(2,1)}, bf16[256,224]{1,0:T(8,128)(2,1)}, bf16[256,224]{1,0:T(8,128)(2,1)}, bf16[2,1,128,224]{3,2,1,0:T(8,128)(2,1)}) custom-call(s32[2]{0:T(128)} %live_ref.1, bf16[2,1,128,224]{3,2,1,0:T(8,128)(2,1)} %copy.17.x_ref, bf16[2,128,224]{2,1,0:T(8,128)(2,1)} %copy.18.loss_ref, ...), custom_call_target="tpu_custom_call" | custom-call | tf_op jit(solution)/shard_map/relay/pallas_call | solution.py:399
  176.6 1.7 copy.24
  178.2 12.5 %update.1 = (bf16[1,224,4096]{2,1,0:T(8,128)(2,1)}, bf16[1,2048,224]{2,1,0:T(8,128)(2,1)}, bf16[1,224,4096]{2,1,0:T(8,128)(2,1)}, bf16[1,2048,224]{2,1,0:T(8,128...) custom-call(bf16[256,4096]{1,0:T(8,128)(2,1)} %get-tuple-element.19.both_ref, ...), custom_call_target="tpu_custom_call" | custom-call | tf_op jit(solution)/shard_map/update/pallas_call | solution.py:441
  190.7 0.0 copy-start.2
  190.7 0.0 copy-start.1
  190.7 2.4 %copy.25 = bf16[1,2048,224]{1,2,0:T(8,128)(2,1)} copy(bf16[1,2048,224]{2,1,0:T(8,128)(2,1)} %get-tuple-element.31) | data formatting | bytes 1835008
  193.1 0.0 copy-done.2
  193.1 1.3 copy.26
  194.4 0.0 copy-done.1
  194.4 1.3 copy.27
Async XLA Ops:
  0.6 7.1 %copy-start.3 = (bf16[1,2048,224]{1,2,0:T(8,128)(2,1)S(1)}, bf16[1,2048,224]{1,2,0:T(8,128)(2,1)}, u32[]{:S(2)}) copy-start(bf16[1,2048,224]{1,2,0:T(8,128)(2,1)} %param.19) | copy-start | bytes 2752516
  5.3 3.7 %copy-start = (bf16[2,1,2048,224]{2,3,1,0:T(8,128)(2,1)S(1)}, bf16[2,1,2048,224]{2,3,1,0:T(8,128)(2,1)}, u32[]{:S(2)}) copy-start(bf16[2,1,2048,224]{2,3,1,0:T(8,128)(2,1)} %param.15) | copy-start | bytes 5505028
  190.7 2.4 %copy-start.2 = (bf16[1,2048,224]{2,1,0:T(8,128)(2,1)S(1)}, bf16[1,2048,224]{2,1,0:T(8,128)(2,1)}, u32[]{:S(2)}) copy-start(bf16[1,2048,224]{2,1,0:T(8,128)(2,1)} %get-tuple-element.33) | copy-start | bytes 2752516
  190.7 3.6 %copy-start.1 = (bf16[1,2048,224]{2,1,0:T(8,128)(2,1)S(1)}, bf16[1,2048,224]{2,1,0:T(8,128)(2,1)}, u32[]{:S(2)}) copy-start(bf16[1,2048,224]{2,1,0:T(8,128)(2,1)} %get-tuple-element.35) | copy-start | bytes 2752516

commit v2 on v1

v2 whole, which is shorter than its diff:
```python
import functools

import jax
import jax.numpy as jnp
from jax import lax
from jax.experimental import pallas as pl
from jax.experimental.pallas import tpu as pltpu
from jax.sharding import PartitionSpec as P

rms_eps = 1e-06
beta_first = 0.9
beta_second = 0.95
learn_rate = 0.00022
decay_rate = 0.1
adam_eps = 1e-08

BF16 = jnp.bfloat16
F32 = jnp.float32
LANES = 128

PRE_SUM, PRE_ALL, GRAD_SUM, GRAD_ALL, HAND = 0, 2, 4, 6, 8
STATS, MIR_GAINED, MIR_OUT, MIR_PRE, MIR_GRAD, MIR_RMS = 10, 11, 12, 13, 14, 15


def dot_nt(left, right):
    return lax.dot_general(left, right, (((1,), (1,)), ((), ())), preferred_element_type=F32)


def await_bytes(ref, sem):
    pltpu.make_async_copy(ref, ref, sem).wait()


def relay_kernel(
    n,
    live_ref,
    x_ref,
    loss_ref,
    gain_ref,
    win_ref,
    wout_ref,
    both_ref,
    hid_ref,
    gained_ref,
    gout_ref,
    gin_ref,
    gained_s,
    gain_s,
    pre_send,
    pre_recv,
    pre_full,
    grad_send,
    grad_recv,
    grad_full,
    stat_all,
    rms_s,
    gate_coef,
    up_coef,
    dot_coef,
    hand,
    next_s,
    gained_mir,
    out_mir,
    send_sems,
    recv_sems,
):
    pipe = lax.axis_index("pipe")
    me = lax.axis_index("dp")
    high = pipe // 2
    inner = (pipe * (3 - pipe)) // 2
    section = (1 - high, high)
    half = n // 2
    local, tokens = x_ref.shape[2:]
    rows = tokens // 2
    hidden = wout_ref.shape[3]
    width = n * local
    chunks = hidden // 256
    across = lax.rem(me + half, n)

    barrier = pltpu.get_barrier_semaphore()

    def greet(step, carry):
        pl.semaphore_signal(barrier, inc=1, device_id={"dp": lax.rem(me + step, n)})
        return carry

    def greet_mirror(step, carry):
        pl.semaphore_signal(
            barrier, inc=1, device_id={"pipe": 3 - pipe, "dp": lax.rem(me + step, n)}
        )
        return carry

    lax.fori_loop(1, n, greet, 0)
    lax.fori_loop(0, n, greet_mirror, 0)
    pl.semaphore_signal(barrier, inc=1, device_id={"pipe": lax.rem(pipe + 1, 4)})
    pl.semaphore_signal(barrier, inc=1, device_id={"pipe": lax.rem(pipe + 2, 4)})
    pl.semaphore_signal(barrier, inc=1, device_id={"pipe": lax.rem(pipe + 3, 4)})

    def remote(source, target, slot, where):
        pltpu.make_async_remote_copy(
            src_ref=source,
            dst_ref=target,
            send_sem=send_sems.at[slot],
            recv_sem=recv_sems.at[slot],
            device_id=where,
        ).start()

    def spread(source, target, slot):
        def one(step, carry):
            peer = lax.rem(me + step, n)
            remote(source(peer), target, slot, {"dp": peer})
            return carry

        lax.fori_loop(1, n, one, 0)

    def gain_inputs(k):
        inputs_t = x_ref[section[k], 0].astype(F32)
        gains_f = gain_ref[...].astype(F32)
        gain = jnp.where(section[k] == 0, gains_f[0:1, :], gains_f[1:2, :])
        gain_s[k] = jnp.transpose(jnp.broadcast_to(gain, (LANES, local)))
        gained_s[k] = (gain_s[k] * inputs_t).astype(BF16)
        stat_all[me, pl.ds(8 * k, 8), :] = lax.dot_general(
            jnp.ones((8, local), F32),
            inputs_t * inputs_t,
            (((1,), (0,)), ((), ())),
            preferred_element_type=F32,
            precision=lax.Precision.HIGHEST,
        )

    def pre_partial(k):
        gained = jnp.transpose(gained_s[k].astype(F32)).astype(BF16)

        def chunk(c, carry):
            for part in range(2):
                columns = pl.ds(pl.multiple_of(part * hidden + c * 256, 256), 256)
                sums = jnp.dot(
                    gained, win_ref[section[k], 0, :, columns], preferred_element_type=F32
                ).astype(BF16)
                for q in range(2):
                    for th in range(2):
                        pre_send[k, th * half + 2 * c + q, part] = sums[
                            th * rows : (th + 1) * rows, q * LANES : (q + 1) * LANES
                        ]
            return carry

        lax.fori_loop(0, chunks, chunk, 0)
        pre_recv[k, me] = pre_send[k, me]

    def pre_scatter(k):
        spread(lambda peer: pre_send.at[k, peer], pre_recv.at[k, me], PRE_SUM + k)

    def pre_reduce(k):
        await_bytes(pre_recv.at[k, pl.ds(0, n - 1)], recv_sems.at[PRE_SUM + k])
        for part in range(2):
            total = lax.fori_loop(
                0,
                n,
                lambda j, acc: acc + pre_recv[k, j, part].astype(F32),
                jnp.zeros((rows, LANES), F32),
            )
            pre_full[k, me, part] = total.astype(BF16)
        spread(lambda peer: pre_full.at[k, me], pre_full.at[k, me], PRE_ALL + k)

    def coefficients(k, row_at):
        for th in range(2):
            scale = rms_s[k, pl.ds(th * rows, rows), :]

            def block(fb, carry):
                j = th * half + fb
                gate_pre = pre_full[k, j, 0].astype(F32)
                up_pre = pre_full[k, j, 1].astype(F32)
                gate_val = scale * gate_pre
                up_val = scale * up_pre
                sigma = jax.nn.sigmoid(gate_val)
                swish = gate_val * sigma
                for_gate = scale * up_val * sigma * (1.0 + gate_val * (1.0 - sigma))
                for_up = scale * swish
                gate_coef[k, j] = for_gate
                up_coef[k, j] = for_up
                dot_coef[k, j] = for_gate * gate_pre + for_up * up_pre
                hid_ref[
                    pl.ds(row_at + th * rows, rows), pl.ds(pl.multiple_of(fb * LANES, LANES), LANES)
                ] = (swish * up_val).astype(BF16)
                return carry

            lax.fori_loop(0, half, block, 0)

    def pre_finish(k):
        await_bytes(pre_full.at[k, pl.ds(0, n - 1)], recv_sems.at[PRE_ALL + k])
        coefficients(k, pl.multiple_of(section[k] * tokens, tokens))

        @pl.when(section[k] == 1)
        def _():
            remote(pre_full.at[k], pre_full.at[2], MIR_PRE, {"pipe": 3 - pipe, "dp": across})

    def both_grads(k, row_at):
        dots = []
        for th in range(2):

            def block(fb, acc):
                j = th * half + fb
                grad_hidden = grad_full[k, j].astype(F32)
                at = pl.ds(row_at + th * rows, rows)
                both_ref[at, pl.ds(pl.multiple_of(fb * LANES, LANES), LANES)] = (
                    grad_hidden * gate_coef[k, j]
                ).astype(BF16)
                both_ref[at, pl.ds(pl.multiple_of(hidden + fb * LANES, LANES), LANES)] = (
                    grad_hidden * up_coef[k, j]
                ).astype(BF16)
                return acc + grad_hidden * dot_coef[k, j]

            dots.append(lax.fori_loop(0, half, block, jnp.zeros((rows, LANES), F32)))
        return jnp.concatenate(dots, axis=0)

    def grad_scatter(k):
        grad_out = jnp.transpose(hand[k].astype(F32)).astype(BF16)

        def chunk(c, carry):
            columns = pl.ds(pl.multiple_of(c * 256, 256), 256)
            sums = jnp.dot(
                grad_out, wout_ref[section[k], 0, :, columns], preferred_element_type=F32
            ).astype(BF16)
            for q in range(2):
                for th in range(2):
                    grad_send[k, th * half + 2 * c + q] = sums[
                        th * rows : (th + 1) * rows, q * LANES : (q + 1) * LANES
                    ]
            return carry

        lax.fori_loop(0, chunks, chunk, 0)
        grad_recv[k, me] = grad_send[k, me]
        spread(lambda peer: grad_send.at[k, peer], grad_recv.at[k, me], GRAD_SUM + k)

    def grad_reduce(k):
        await_bytes(grad_recv.at[k, pl.ds(0, n - 1)], recv_sems.at[GRAD_SUM + k])
        total = lax.fori_loop(
            0,
            n,
            lambda j, acc: acc + grad_recv[k, j].astype(F32),
            jnp.zeros((rows, LANES), F32),
        )
        grad_full[k, me] = total.astype(BF16)
        spread(lambda peer: grad_full.at[k, me], grad_full.at[k, me], GRAD_ALL + k)
        if k == 1:

            @pl.when(section[k] == 1)
            def _():
                def one(step, carry):
                    peer = lax.rem(me + step, n)
                    remote(
                        grad_full.at[k, me],
                        grad_full.at[2, me],
                        MIR_GRAD,
                        {"pipe": 3 - pipe, "dp": peer},
                    )
                    return carry

                lax.fori_loop(0, n, one, 0)

    def grad_finish(k):
        sec = section[k]
        await_bytes(grad_full.at[k, pl.ds(0, n - 1)], recv_sems.at[GRAD_ALL + k])

        @pl.when(sec == 1)
        def _():
            if k == 0:
                remote(grad_full.at[k], grad_full.at[2], MIR_GRAD, {"pipe": 3 - pipe, "dp": across})
            remote(hand.at[k], out_mir, MIR_OUT, {"pipe": 3 - pipe})

        row_at = pl.multiple_of(sec * tokens, tokens)
        hidden_dot = lax.dot_general(
            jnp.ones((8, LANES), F32),
            both_grads(k, row_at),
            (((1,), (1,)), ((), ())),
            preferred_element_type=F32,
            precision=lax.Precision.HIGHEST,
        )

        def part(c, acc):
            columns = pl.ds(pl.multiple_of(c * 512, 512), 512)
            return acc + dot_nt(win_ref[sec, 0, :, columns], both_ref[pl.ds(row_at, tokens), columns])

        grad_gained = lax.fori_loop(0, 2 * hidden // 512, part, jnp.zeros((local, tokens), F32))
        row_coef = (mean_factor(k) * hidden_dot)[0:1, :]
        grad_in = (
            hand[k].astype(F32)
            + gain_s[k] * grad_gained
            - x_ref[sec, 0].astype(F32) * row_coef
        ).astype(BF16)
        gin_ref[sec, 0] = grad_in
        next_s[k] = grad_in

    def stats_sum(k):
        return lax.fori_loop(
            0,
            n,
            lambda j, acc: acc + stat_all[j, pl.ds(8 * k, 8), :],
            jnp.zeros((8, tokens), F32),
        )

    def mean_factor(k):
        return 1.0 / ((stats_sum(k) / width + rms_eps) * width)

    def rms_finish():
        await_bytes(stat_all.at[pl.ds(0, n - 1)], recv_sems.at[STATS])
        for k in range(2):
            sum_squares = lax.dot_general(
                stats_sum(k),
                jnp.full((8, LANES), 0.125, F32),
                (((0,), (0,)), ((), ())),
                preferred_element_type=F32,
                precision=lax.Precision.HIGHEST,
            )
            rms_s[k] = lax.rsqrt(sum_squares / width + rms_eps)
        remote(rms_s.at[high], rms_s.at[2], MIR_RMS, {"pipe": 3 - pipe, "dp": across})

    for_inner = pl.when(inner == 1)
    for_outer = pl.when(inner == 0)

    gain_inputs(0)
    gain_inputs(1)
    pre_partial(0)
    pl.semaphore_wait(barrier, 2 * n + 2)
    pre_scatter(0)
    spread(lambda peer: stat_all.at[me], stat_all.at[me], STATS)

    @for_outer
    def _():
        token_ids = lax.broadcasted_iota(jnp.int32, (local, tokens), 1)
        start = loss_ref[section[0]]
        live = jnp.where(section[0] == 0, live_ref[0], live_ref[1])
        hand[0] = jnp.where(token_ids < live, start, jnp.zeros_like(start))
        grad_scatter(0)

    remote(gained_s.at[high], gained_mir, MIR_GAINED, {"pipe": 3 - pipe})
    pre_partial(1)
    pre_reduce(0)
    rms_finish()

    @for_outer
    def _():
        grad_reduce(0)

    @for_inner
    def _():
        pre_scatter(1)

    pre_finish(0)

    @for_outer
    def _():
        grad_finish(0)
        remote(next_s.at[0], hand.at[0], HAND, {"pipe": pipe + 1 - 2 * high})
        pre_scatter(1)
        pre_reduce(1)
        pre_finish(1)

    @for_inner
    def _():
        await_bytes(hand.at[0], recv_sems.at[HAND])
        grad_scatter(0)
        grad_reduce(0)
        pre_reduce(1)
        grad_finish(0)
        remote(next_s.at[0], hand.at[1], HAND + 1, {"pipe": pipe + 1 - 2 * high})
        pre_finish(1)

    await_bytes(hand.at[1], recv_sems.at[HAND + 1])
    grad_scatter(1)
    gained_ref[:, pl.ds(0, tokens)] = gained_s[1 - high]
    await_bytes(gained_mir, recv_sems.at[MIR_GAINED])
    gained_ref[:, pl.ds(tokens, tokens)] = gained_mir[...]
    gout_ref[:, pl.ds(0, tokens)] = hand[1 - high]
    grad_reduce(1)
    grad_finish(1)

    @for_inner
    def _():
        remote(next_s.at[1], hand.at[1], HAND + 1, {"pipe": pipe - 1 + 2 * high})

    await_bytes(rms_s.at[2], recv_sems.at[MIR_RMS])
    await_bytes(pre_full.at[2], recv_sems.at[MIR_PRE])
    coefficients(2, tokens)
    await_bytes(grad_full.at[2], recv_sems.at[MIR_GRAD])
    both_grads(2, tokens)
    await_bytes(out_mir, recv_sems.at[MIR_OUT])
    gout_ref[:, pl.ds(tokens, tokens)] = out_mir[...]

    for k in range(2):
        await_bytes(pre_send.at[k, pl.ds(0, n - 1)], send_sems.at[PRE_SUM + k])
        await_bytes(pre_full.at[k, pl.ds(0, n - 1)], send_sems.at[PRE_ALL + k])
        await_bytes(grad_send.at[k, pl.ds(0, n - 1)], send_sems.at[GRAD_SUM + k])
        await_bytes(grad_full.at[k, pl.ds(0, n - 1)], send_sems.at[GRAD_ALL + k])
    await_bytes(stat_all.at[pl.ds(0, n - 1)], send_sems.at[STATS])
    await_bytes(gained_mir, send_sems.at[MIR_GAINED])
    await_bytes(out_mir, send_sems.at[MIR_OUT])
    await_bytes(pre_full.at[2], send_sems.at[MIR_PRE])
    await_bytes(grad_full.at[2], send_sems.at[MIR_GRAD])
    await_bytes(rms_s.at[2], send_sems.at[MIR_RMS])

    @for_outer
    def _():
        await_bytes(next_s.at[0], send_sems.at[HAND])

    @for_inner
    def _():
        await_bytes(next_s, send_sems.at[HAND + 1])


def adamw(weights, first, second, grads):
    first_new = beta_first * first.astype(F32) + (1.0 - beta_first) * grads
    second_new = beta_second * second.astype(F32) + (1.0 - beta_second) * grads * grads
    weights_f = weights.astype(F32)
    weights_new = weights_f - learn_rate * (
        first_new / (jnp.sqrt(second_new) + adam_eps) + decay_rate * weights_f
    )
    return (weights_new.astype(BF16), first_new.astype(BF16), second_new.astype(BF16))


def update_kernel(
    both_ref,
    hid_ref,
    gained_ref,
    gout_ref,
    win_ref,
    wout_ref,
    fin_ref,
    fout_ref,
    sin_ref,
    sout_ref,
    nwin_ref,
    nwout_ref,
    nfin_ref,
    nfout_ref,
    nsin_ref,
    nsout_ref,
):
    grad_in = jnp.dot(gained_ref[...], both_ref[...], preferred_element_type=F32)
    nwin_ref[0], nfin_ref[0], nsin_ref[0] = adamw(
        win_ref[0, 0], fin_ref[0], sin_ref[0], grad_in
    )
    grad_out = jnp.dot(gout_ref[...], hid_ref[...], preferred_element_type=F32)
    nwout_ref[0], nfout_ref[0], nsout_ref[0] = adamw(
        wout_ref[0, 0], fout_ref[0], sout_ref[0], grad_out
    )


def shards(
    section_inputs,
    loss_grads,
    live_tokens,
    gains,
    w_in,
    w_out,
    first_in,
    first_out,
    second_in,
    second_out,
):
    n = lax.axis_size("dp")
    flip = lambda array: jnp.swapaxes(array, -1, -2)
    x_t, loss_t, wout_t = flip(section_inputs), flip(loss_grads), flip(w_out)
    fout_t, sout_t = flip(first_out), flip(second_out)
    local, tokens = x_t.shape[2:]
    hidden = wout_t.shape[3]
    rows = tokens // 2
    vmem = pl.BlockSpec(memory_space=pltpu.VMEM)
    blocks = (n, rows, LANES)
    both, hid, gained, gout, gin = pl.pallas_call(
        functools.partial(relay_kernel, n),
        out_shape=(
            jax.ShapeDtypeStruct((2 * tokens, 2 * hidden), BF16),
            jax.ShapeDtypeStruct((2 * tokens, hidden), BF16),
            jax.ShapeDtypeStruct((local, 2 * tokens), BF16),
            jax.ShapeDtypeStruct((local, 2 * tokens), BF16),
            jax.ShapeDtypeStruct(x_t.shape, BF16),
        ),
        in_specs=[pl.BlockSpec(memory_space=pltpu.SMEM)] + [vmem] * 5,
        out_specs=(vmem,) * 5,
        scratch_shapes=[
            pltpu.VMEM((2, local, tokens), BF16),
            pltpu.VMEM((2, local, tokens), F32),
            pltpu.VMEM((2, n, 2, rows, LANES), BF16),
            pltpu.VMEM((2, n, 2, rows, LANES), BF16),
            pltpu.VMEM((3, n, 2, rows, LANES), BF16),
            pltpu.VMEM((2,) + blocks, BF16),
            pltpu.VMEM((2,) + blocks, BF16),
            pltpu.VMEM((3,) + blocks, BF16),
            pltpu.VMEM((n, 16, tokens), F32),
            pltpu.VMEM((3, tokens, LANES), F32),
            pltpu.VMEM((3,) + blocks, F32),
            pltpu.VMEM((3,) + blocks, F32),
            pltpu.VMEM((3,) + blocks, F32),
            pltpu.VMEM((2, local, tokens), BF16),
            pltpu.VMEM((2, local, tokens), BF16),
            pltpu.VMEM((local, tokens), BF16),
            pltpu.VMEM((local, tokens), BF16),
            pltpu.SemaphoreType.DMA((16,)),
            pltpu.SemaphoreType.DMA((16,)),
        ],
        compiler_params=pltpu.CompilerParams(
            collective_id=0, has_side_effects=True, vmem_limit_bytes=60 * 1024 * 1024
        ),
        name="relay",
    )(live_tokens, x_t, loss_t, jnp.reshape(gains, (2, local)), w_in, wout_t)

    steps = 8
    wide, tall = 2 * hidden // steps, hidden // steps
    in_block = pl.BlockSpec((1, local, wide), lambda i: (0, 0, i))
    out_block = pl.BlockSpec((1, local, tall), lambda i: (0, 0, i))
    whole = pl.BlockSpec((local, 2 * tokens), lambda i: (0, 0))
    new_in, new_out, mom_in, mom_out, sec_in, sec_out = pl.pallas_call(
        update_kernel,
        grid=(steps,),
        out_shape=tuple(
            jax.ShapeDtypeStruct(a.shape, BF16)
            for a in (first_in, fout_t, first_in, fout_t, second_in, sout_t)
        ),
        in_specs=[
            pl.BlockSpec((2 * tokens, wide), lambda i: (0, i)),
            pl.BlockSpec((2 * tokens, tall), lambda i: (0, i)),
            whole,
            whole,
            pl.BlockSpec((1, 1, local, wide), lambda i: (0, 0, 0, i)),
            pl.BlockSpec((1, 1, local, tall), lambda i: (0, 0, 0, i)),
            in_block,
            out_block,
            in_block,
            out_block,
        ],
        out_specs=(in_block, out_block) * 3,
        compiler_params=pltpu.CompilerParams(vmem_limit_bytes=60 * 1024 * 1024),
        name="update",
    )(both, hid, gained, gout, w_in, wout_t, first_in, fout_t, second_in, sout_t)
    return (flip(gin), new_in, flip(new_out), mom_in, flip(mom_out), sec_in, flip(sec_out))


def solution(mesh):
    placed = (
        P(None, "pipe", None, "dp"),
        P(None, None, "dp"),
        P(),
        P(None, "pipe", "dp"),
        P(None, "pipe", "dp", None),
        P(None, "pipe", None, "dp"),
        P("pipe", "dp", None),
        P("pipe", None, "dp"),
        P("pipe", "dp", None),
        P("pipe", None, "dp"),
    )
    return jax.shard_map(
        shards,
        mesh=mesh,
        in_specs=placed,
        out_specs=(
            P(None, "pipe", None, "dp"),
            P("pipe", "dp", None),
            P("pipe", None, "dp"),
            P("pipe", "dp", None),
            P("pipe", None, "dp"),
            P("pipe", "dp", None),
            P("pipe", None, "dp"),
        ),
        check_vma=False,
    )
```

time: 196 us -> 148 us (0.76)
  Pallas kernels: 178 us -> 147 us
  local copies, waits for them, and re-layouts: 17.3 us -> 0.65 us
    pallas_call x1, Pallas kernels: 165 us -> 134 us  [shards(): pl.pallas_call(functools.partial(relay_kernel, n), out_shape=(jax.ShapeDt...]
    unnamed x18 -> x3, local copies, waits for them, and re-layouts: 17.3 us -> 0.65 us
where the time goes in v2:
time: 148 us
  Pallas kernels  147 us (99%)
    pallas_call x1, Pallas kernels, shards(): pl.pallas_call(functools.partial(relay_kernel, n), out_shape=(jax.ShapeDt...  134 us
    pallas_call x1, Pallas kernels, shards(): pl.pallas_call(update_kernel, grid=(steps,), out_shape=tuple((jax.ShapeDt...  12.3 us

profile of v2, /device:TPU:0, one launch (start us, length us, event | category | flops | bytes accessed | tf_op | source)
XLA Modules:
  0.0 148.0 jit_solution(1062181975146051799)
XLA Ops:
  0.6 134.4 %relay.1 = (bf16[256,4096]{1,0:T(8,128)(2,1)}, bf16[256,2048]{1,0:T(8,128)(2,1)}, bf16[224,256]{1,0:T(8,128)(2,1)}, bf16[224,256]{1,0:T(8,128)(2,1)}, bf16[2,1,224,128]{3,2,1,0:T(8,128)(2,1)}) custom-call(s32[2]{0:T(128)} %live_ref.1, bf16[2,1,224,128]{3,2,1,0:T(8,128)(2,1)} %bitcast.15, bf16[2,224,128]{2,1,0:T(8,128)(2,1)} %bitcast.16, ...), custom_call_target="tpu_custom_call" | custom-call | tf_op jit(solution)/shard_map/relay/pallas_call | solution.py:467
  135.0 0.0 copy-start
  135.1 12.3 %update.1 = (bf16[1,224,4096]{2,1,0:T(8,128)(2,1)}, bf16[1,224,2048]{2,1,0:T(8,128)(2,1)}, bf16[1,224,4096]{2,1,0:T(8,128)(2,1)}, bf16[1,224,2048]{2,1,0:T(8,128...) custom-call(bf16[256,4096]{1,0:T(8,128)(2,1)} %get-tuple-element.19.both_ref, ...), custom_call_target="tpu_custom_call" | custom-call | tf_op jit(solution)/shard_map/update/pallas_call | solution.py:510
  147.3 0.0 copy-done
  147.3 0.6 copy.18
Async XLA Ops:
  135.0 12.3 %copy-start = (bf16[2,1,224,128]{3,2,1,0:T(8,128)(2,1)S(1)}, bf16[2,1,224,128]{3,2,1,0:T(8,128)(2,1)}, u32[]{:S(2)}) copy-start(bf16[2,1,224,128]{3,2,1,0:T(8,128)(2,1)} %get-tuple-element.18) | copy-start | bytes 344068

commit v3 on v2

--- a/solution.py
+++ b/solution.py
@@ -18,8 +18,9 @@
 F32 = jnp.float32
 LANES = 128
 
-PRE_SUM, PRE_ALL, GRAD_SUM, GRAD_ALL, HAND = 0, 2, 4, 6, 8
-STATS, MIR_GAINED, MIR_OUT, MIR_PRE, MIR_GRAD, MIR_RMS = 10, 11, 12, 13, 14, 15
+PRE_SUM, PRE_ALL, GRAD_SUM, GRAD_ALL, HAND = 0, 2, 4, 8, 12
+STATS, MIR_GAINED, MIR_OUT, MIR_PRE, MIR_GRAD, MIR_RMS = 16, 17, 18, 19, 20, 22
+SLOTS = 23
 
 
 def dot_nt(left, right):
@@ -44,7 +45,7 @@
     gout_ref,
     gin_ref,
     gained_s,
-    gain_s,
+    inputs_s,
     pre_send,
     pre_recv,
     pre_full,
@@ -71,6 +72,7 @@
     half = n // 2
     local, tokens = x_ref.shape[2:]
     rows = tokens // 2
+    part_rows = rows // 2
     hidden = wout_ref.shape[3]
     width = n * local
     chunks = hidden // 256
@@ -103,20 +105,43 @@
             device_id=where,
         ).start()
 
+    digits = (2, 1, 3, 0)
+
+    def visit(send, everyone):
+        if n != 32:
+            for step in range(1, n + 1 if everyone else n):
+                send(lax.rem(me + step, n))
+            return
+        along = [lax.rem(me + d, 4) for d in digits]
+
+        def base(step):
+            over = lax.rem(2 + 3 * step + (step // 2) * (2 * step - 1), 4)
+            return over
+
+        def group(step, carry):
+            line = lax.rem(step, 4)
+            down = lax.rem(me // 16 + 1 - step // 4, 2)
+            over = lax.rem(me // 4 + base(line), 4)
+            for at in along:
+                send(16 * down + 4 * over + at)
+            return carry
+
+        lax.fori_loop(0, 7, group, 0)
+        for at in along if everyone else along[:3]:
+            send(16 * (me // 16) + 4 * lax.rem(me // 4, 4) + at)
+
     def spread(source, target, slot):
-        def one(step, carry):
-            peer = lax.rem(me + step, n)
-            remote(source(peer), target, slot, {"dp": peer})
-            return carry
-
-        lax.fori_loop(1, n, one, 0)
+        visit(lambda peer: remote(source(peer), target, slot, {"dp": peer}), False)
+
+    def gain_row(k):
+        gains_f = gain_ref[...].astype(F32)
+        return jnp.where(section[k] == 0, gains_f[0:1, :], gains_f[1:2, :])
 
     def gain_inputs(k):
         inputs_t = x_ref[section[k], 0].astype(F32)
-        gains_f = gain_ref[...].astype(F32)
-        gain = jnp.where(section[k] == 0, gains_f[0:1, :], gains_f[1:2, :])
-        gain_s[k] = jnp.transpose(jnp.broadcast_to(gain, (LANES, local)))
-        gained_s[k] = (gain_s[k] * inputs_t).astype(BF16)
+        inputs_f = jnp.transpose(inputs_t)
+        inputs_s[k] = inputs_f
+        gained_s[k] = (gain_row(k) * inputs_f).astype(BF16)
         stat_all[me, pl.ds(8 * k, 8), :] = lax.dot_general(
             jnp.ones((8, local), F32),
             inputs_t * inputs_t,
@@ -126,7 +151,7 @@
         )
 
     def pre_partial(k):
-        gained = jnp.transpose(gained_s[k].astype(F32)).astype(BF16)
+        gained = gained_s[k]
 
         def chunk(c, carry):
             for part in range(2):
@@ -155,6 +180,7 @@
                 n,
                 lambda j, acc: acc + pre_recv[k, j, part].astype(F32),
                 jnp.zeros((rows, LANES), F32),
+                unroll=4,
             )
             pre_full[k, me, part] = total.astype(BF16)
         spread(lambda peer: pre_full.at[k, me], pre_full.at[k, me], PRE_ALL + k)
@@ -181,7 +207,7 @@
                 ] = (swish * up_val).astype(BF16)
                 return carry
 
-            lax.fori_loop(0, half, block, 0)
+            lax.fori_loop(0, half, block, 0, unroll=2)
 
     def pre_finish(k):
         await_bytes(pre_full.at[k, pl.ds(0, n - 1)], recv_sems.at[PRE_ALL + k])
@@ -191,102 +217,92 @@
         def _():
             remote(pre_full.at[k], pre_full.at[2], MIR_PRE, {"pipe": 3 - pipe, "dp": across})
 
-    def both_grads(k, row_at):
+    def both_grads(k, h, row_at):
         dots = []
-        for th in range(2):
+        for tq in range(2):
+            inside = pl.ds(tq * part_rows, part_rows)
+            at = pl.ds(row_at + h * rows + tq * part_rows, part_rows)
 
             def block(fb, acc):
-                j = th * half + fb
-                grad_hidden = grad_full[k, j].astype(F32)
-                at = pl.ds(row_at + th * rows, rows)
+                grad_hidden = grad_full[k, h, tq * half + fb].astype(F32)
+                j = h * half + fb
                 both_ref[at, pl.ds(pl.multiple_of(fb * LANES, LANES), LANES)] = (
-                    grad_hidden * gate_coef[k, j]
+                    grad_hidden * gate_coef[k, j, inside, :]
                 ).astype(BF16)
                 both_ref[at, pl.ds(pl.multiple_of(hidden + fb * LANES, LANES), LANES)] = (
-                    grad_hidden * up_coef[k, j]
+                    grad_hidden * up_coef[k, j, inside, :]
                 ).astype(BF16)
-                return acc + grad_hidden * dot_coef[k, j]
-
-            dots.append(lax.fori_loop(0, half, block, jnp.zeros((rows, LANES), F32)))
+                return acc + grad_hidden * dot_coef[k, j, inside, :]
+
+            acc = lax.fori_loop(
+                0, half, block, jnp.zeros((part_rows, LANES), F32), unroll=True
+            )
+            dots.append(jnp.sum(acc, axis=1, keepdims=True))
         return jnp.concatenate(dots, axis=0)
 
-    def grad_scatter(k):
-        grad_out = jnp.transpose(hand[k].astype(F32)).astype(BF16)
-
-        def chunk(c, carry):
-            columns = pl.ds(pl.multiple_of(c * 256, 256), 256)
-            sums = jnp.dot(
-                grad_out, wout_ref[section[k], 0, :, columns], preferred_element_type=F32
-            ).astype(BF16)
-            for q in range(2):
-                for th in range(2):
-                    grad_send[k, th * half + 2 * c + q] = sums[
-                        th * rows : (th + 1) * rows, q * LANES : (q + 1) * LANES
-                    ]
-            return carry
-
-        lax.fori_loop(0, chunks, chunk, 0)
-        grad_recv[k, me] = grad_send[k, me]
-        spread(lambda peer: grad_send.at[k, peer], grad_recv.at[k, me], GRAD_SUM + k)
-
-    def grad_reduce(k):
-        await_bytes(grad_recv.at[k, pl.ds(0, n - 1)], recv_sems.at[GRAD_SUM + k])
+    def grad_scatter(k, h):
+        grad_out = hand[k, h]
+
+        sums = jnp.dot(grad_out, wout_ref[section[k], 0], preferred_element_type=F32).astype(BF16)
+        for q in range(half):
+            for tq in range(2):
+                grad_send[k, h, tq * half + q] = sums[
+                    tq * part_rows : (tq + 1) * part_rows, q * LANES : (q + 1) * LANES
+                ]
+        grad_recv[k, h, me] = grad_send[k, h, me]
+        spread(
+            lambda peer: grad_send.at[k, h, peer], grad_recv.at[k, h, me], GRAD_SUM + 2 * k + h
+        )
+
+    def grad_reduce(k, h):
+        await_bytes(grad_recv.at[k, h, pl.ds(0, n - 1)], recv_sems.at[GRAD_SUM + 2 * k + h])
         total = lax.fori_loop(
             0,
             n,
-            lambda j, acc: acc + grad_recv[k, j].astype(F32),
-            jnp.zeros((rows, LANES), F32),
+            lambda j, acc: acc + grad_recv[k, h, j].astype(F32),
+            jnp.zeros((part_rows, LANES), F32),
+            unroll=True,
         )
-        grad_full[k, me] = total.astype(BF16)
-        spread(lambda peer: grad_full.at[k, me], grad_full.at[k, me], GRAD_ALL + k)
+        grad_full[k, h, me] = total.astype(BF16)
+        mine = grad_full.at[k, h, me]
+        spread(lambda peer: mine, mine, GRAD_ALL + 2 * k + h)
         if k == 1:
 
             @pl.when(section[k] == 1)
             def _():
-                def one(step, carry):
-                    peer = lax.rem(me + step, n)
-                    remote(
-                        grad_full.at[k, me],
-                        grad_full.at[2, me],
-                        MIR_GRAD,
-                        {"pipe": 3 - pipe, "dp": peer},
-                    )
-                    return carry
-
-                lax.fori_loop(0, n, one, 0)
-
-    def grad_finish(k):
+                def one(peer):
+                    where = {"pipe": 3 - pipe, "dp": peer}
+                    remote(mine, grad_full.at[2, h, me], MIR_GRAD + h, where)
+
+                visit(one, True)
+
+    def grad_finish(k, h):
         sec = section[k]
-        await_bytes(grad_full.at[k, pl.ds(0, n - 1)], recv_sems.at[GRAD_ALL + k])
-
-        @pl.when(sec == 1)
+        await_bytes(grad_full.at[k, h, pl.ds(0, n - 1)], recv_sems.at[GRAD_ALL + 2 * k + h])
+        row_at = pl.multiple_of(sec * tokens, tokens)
+        hidden_dot = both_grads(k, h, row_at)
+        at = pl.ds(pl.multiple_of(row_at + h * rows, rows), rows)
+
+        grad_gained = dot_nt(both_ref[at, :], win_ref[sec, 0])
+        inv_rms = rms_s[k, pl.ds(h * rows, rows), 0:1]
+        row_coef = inv_rms * inv_rms * hidden_dot / width
+        next_s[k, h] = (
+            hand[k, h].astype(F32)
+            + gain_row(k) * grad_gained
+            - inputs_s[k, pl.ds(h * rows, rows), :] * row_coef
+        ).astype(BF16)
+
+    def mirror_grads(k):
+        @pl.when(section[k] == 1)
         def _():
             if k == 0:
-                remote(grad_full.at[k], grad_full.at[2], MIR_GRAD, {"pipe": 3 - pipe, "dp": across})
+                for h in range(2):
+                    where = {"pipe": 3 - pipe, "dp": across}
+                    remote(grad_full.at[k, h], grad_full.at[2, h], MIR_GRAD + h, where)
             remote(hand.at[k], out_mir, MIR_OUT, {"pipe": 3 - pipe})
 
-        row_at = pl.multiple_of(sec * tokens, tokens)
-        hidden_dot = lax.dot_general(
-            jnp.ones((8, LANES), F32),
-            both_grads(k, row_at),
-            (((1,), (1,)), ((), ())),
-            preferred_element_type=F32,
-            precision=lax.Precision.HIGHEST,
-        )
-
-        def part(c, acc):
-            columns = pl.ds(pl.multiple_of(c * 512, 512), 512)
-            return acc + dot_nt(win_ref[sec, 0, :, columns], both_ref[pl.ds(row_at, tokens), columns])
-
-        grad_gained = lax.fori_loop(0, 2 * hidden // 512, part, jnp.zeros((local, tokens), F32))
-        row_coef = (mean_factor(k) * hidden_dot)[0:1, :]
-        grad_in = (
-            hand[k].astype(F32)
-            + gain_s[k] * grad_gained
-            - x_ref[sec, 0].astype(F32) * row_coef
-        ).astype(BF16)
-        gin_ref[sec, 0] = grad_in
-        next_s[k] = grad_in
+    def flipped(halves):
+        return jnp.transpose(jnp.concatenate([halves[0], halves[1]], axis=0).astype(F32)).astype(BF16)
 
     def stats_sum(k):
         return lax.fori_loop(
@@ -295,9 +311,6 @@
             lambda j, acc: acc + stat_all[j, pl.ds(8 * k, 8), :],
             jnp.zeros((8, tokens), F32),
         )
-
-    def mean_factor(k):
-        return 1.0 / ((stats_sum(k) / width + rms_eps) * width)
 
     def rms_finish():
         await_bytes(stat_all.at[pl.ds(0, n - 1)], recv_sems.at[STATS])
@@ -317,27 +330,40 @@
 
     gain_inputs(0)
     gain_inputs(1)
+
+    @for_outer
+    def _():
+        token_ids = lax.broadcasted_iota(jnp.int32, (tokens, local), 0)
+        start = jnp.transpose(loss_ref[section[0]].astype(F32))
+        live = jnp.where(section[0] == 0, live_ref[0], live_ref[1])
+        masked = jnp.where(token_ids < live, start, jnp.zeros_like(start)).astype(BF16)
+        hand[0, 0] = masked[:rows]
+        hand[0, 1] = masked[rows:]
+
     pre_partial(0)
     pl.semaphore_wait(barrier, 2 * n + 2)
-    pre_scatter(0)
     spread(lambda peer: stat_all.at[me], stat_all.at[me], STATS)
 
     @for_outer
     def _():
-        token_ids = lax.broadcasted_iota(jnp.int32, (local, tokens), 1)
-        start = loss_ref[section[0]]
-        live = jnp.where(section[0] == 0, live_ref[0], live_ref[1])
-        hand[0] = jnp.where(token_ids < live, start, jnp.zeros_like(start))
-        grad_scatter(0)
+        pre_scatter(0)
+        grad_scatter(0, 0)
+        grad_scatter(0, 1)
+
+    pre_partial(1)
+    rms_finish()
+
+    @for_inner
+    def _():
+        pre_scatter(0)
 
     remote(gained_s.at[high], gained_mir, MIR_GAINED, {"pipe": 3 - pipe})
-    pre_partial(1)
     pre_reduce(0)
-    rms_finish()
 
     @for_outer
     def _():
-        grad_reduce(0)
+        grad_reduce(0, 0)
+        grad_reduce(0, 1)
 
     @for_inner
     def _():
@@ -347,62 +373,95 @@
 
     @for_outer
     def _():
-        grad_finish(0)
-        remote(next_s.at[0], hand.at[0], HAND, {"pipe": pipe + 1 - 2 * high})
+        for h in range(2):
+            grad_finish(0, h)
+            remote(next_s.at[0, h], hand.at[0, h], HAND + h, {"pipe": pipe + 1 - 2 * high})
         pre_scatter(1)
+        mirror_grads(0)
+        gin_ref[section[0], 0] = flipped(next_s[0])
         pre_reduce(1)
         pre_finish(1)
 
     @for_inner
     def _():
-        await_bytes(hand.at[0], recv_sems.at[HAND])
-        grad_scatter(0)
-        grad_reduce(0)
+        for h in range(2):
+            await_bytes(hand.at[0, h], recv_sems.at[HAND + h])
+            grad_scatter(0, h)
+        grad_reduce(0, 0)
+        grad_reduce(0, 1)
         pre_reduce(1)
-        grad_finish(0)
-        remote(next_s.at[0], hand.at[1], HAND + 1, {"pipe": pipe + 1 - 2 * high})
+        for h in range(2):
+            grad_finish(0, h)
+            remote(next_s.at[0, h], hand.at[1, h], HAND + 2 + h, {"pipe": pipe + 1 - 2 * high})
+        mirror_grads(0)
+        gin_ref[section[0], 0] = flipped(next_s[0])
+
+    for h in range(2):
+        await_bytes(hand.at[1, h], recv_sems.at[HAND + 2 + h])
+        grad_scatter(1, h)
+
+    @for_inner
+    def _():
         pre_finish(1)
 
-    await_bytes(hand.at[1], recv_sems.at[HAND + 1])
-    grad_scatter(1)
-    gained_ref[:, pl.ds(0, tokens)] = gained_s[1 - high]
+    @for_outer
+    def _():
+        await_bytes(rms_s.at[2], recv_sems.at[MIR_RMS])
+        await_bytes(pre_full.at[2], recv_sems.at[MIR_PRE])
+        coefficients(2, tokens)
+
+    grad_reduce(1, 0)
+    grad_reduce(1, 1)
+    mirror_grads(1)
     await_bytes(gained_mir, recv_sems.at[MIR_GAINED])
-    gained_ref[:, pl.ds(tokens, tokens)] = gained_mir[...]
-    gout_ref[:, pl.ds(0, tokens)] = hand[1 - high]
-    grad_reduce(1)
-    grad_finish(1)
+    gained_ref[:, pl.ds(0, tokens)] = jnp.transpose(gained_s[1 - high].astype(F32)).astype(BF16)
+    gained_ref[:, pl.ds(tokens, tokens)] = jnp.transpose(gained_mir[...].astype(F32)).astype(BF16)
+    gout_ref[:, pl.ds(0, tokens)] = flipped(hand[1 - high])
+    for h in range(2):
+        grad_finish(1, h)
+
+        @for_inner
+        def _():
+            remote(next_s.at[1, h], hand.at[1, h], HAND + 2 + h, {"pipe": pipe - 1 + 2 * high})
+
+    gin_ref[section[1], 0] = flipped(next_s[1])
 
     @for_inner
     def _():
-        remote(next_s.at[1], hand.at[1], HAND + 1, {"pipe": pipe - 1 + 2 * high})
-
-    await_bytes(rms_s.at[2], recv_sems.at[MIR_RMS])
-    await_bytes(pre_full.at[2], recv_sems.at[MIR_PRE])
-    coefficients(2, tokens)
-    await_bytes(grad_full.at[2], recv_sems.at[MIR_GRAD])
-    both_grads(2, tokens)
+        await_bytes(rms_s.at[2], recv_sems.at[MIR_RMS])
+        await_bytes(pre_full.at[2], recv_sems.at[MIR_PRE])
+        coefficients(2, tokens)
+
+    for h in range(2):
+        await_bytes(grad_full.at[2, h], recv_sems.at[MIR_GRAD + h])
+        both_grads(2, h, tokens)
     await_bytes(out_mir, recv_sems.at[MIR_OUT])
-    gout_ref[:, pl.ds(tokens, tokens)] = out_mir[...]
+    gout_ref[:, pl.ds(tokens, tokens)] = flipped(out_mir[...])
 
     for k in range(2):
         await_bytes(pre_send.at[k, pl.ds(0, n - 1)], send_sems.at[PRE_SUM + k])
         await_bytes(pre_full.at[k, pl.ds(0, n - 1)], send_sems.at[PRE_ALL + k])
-        await_bytes(grad_send.at[k, pl.ds(0, n - 1)], send_sems.at[GRAD_SUM + k])
-        await_bytes(grad_full.at[k, pl.ds(0, n - 1)], send_sems.at[GRAD_ALL + k])
+        for h in range(2):
+            spans = pl.ds(0, n - 1)
+            await_bytes(grad_send.at[k, h, spans], send_sems.at[GRAD_SUM + 2 * k + h])
+            await_bytes(grad_full.at[k, h, spans], send_sems.at[GRAD_ALL + 2 * k + h])
     await_bytes(stat_all.at[pl.ds(0, n - 1)], send_sems.at[STATS])
     await_bytes(gained_mir, send_sems.at[MIR_GAINED])
     await_bytes(out_mir, send_sems.at[MIR_OUT])
     await_bytes(pre_full.at[2], send_sems.at[MIR_PRE])
-    await_bytes(grad_full.at[2], send_sems.at[MIR_GRAD])
     await_bytes(rms_s.at[2], send_sems.at[MIR_RMS])
+    for h in range(2):
+        await_bytes(grad_full.at[2, h], send_sems.at[MIR_GRAD + h])
 
     @for_outer
     def _():
-        await_bytes(next_s.at[0], send_sems.at[HAND])
+        for h in range(2):
+            await_bytes(next_s.at[0, h], send_sems.at[HAND + h])
 
     @for_inner
     def _():
-        await_bytes(next_s, send_sems.at[HAND + 1])
+        for h in range(2):
+            await_bytes(next_s.at[:, h], send_sems.at[HAND + 2 + h])
 
 
 def adamw(weights, first, second, grads):
@@ -464,6 +523,7 @@
     rows = tokens // 2
     vmem = pl.BlockSpec(memory_space=pltpu.VMEM)
     blocks = (n, rows, LANES)
+    halves = (2, n, rows // 2, LANES)
     both, hid, gained, gout, gin = pl.pallas_call(
         functools.partial(relay_kernel, n),
         out_shape=(
@@ -476,25 +536,25 @@
         in_specs=[pl.BlockSpec(memory_space=pltpu.SMEM)] + [vmem] * 5,
         out_specs=(vmem,) * 5,
         scratch_shapes=[
-            pltpu.VMEM((2, local, tokens), BF16),
-            pltpu.VMEM((2, local, tokens), F32),
+            pltpu.VMEM((2, tokens, local), BF16),
+            pltpu.VMEM((2, tokens, local), F32),
             pltpu.VMEM((2, n, 2, rows, LANES), BF16),
             pltpu.VMEM((2, n, 2, rows, LANES), BF16),
             pltpu.VMEM((3, n, 2, rows, LANES), BF16),
-            pltpu.VMEM((2,) + blocks, BF16),
-            pltpu.VMEM((2,) + blocks, BF16),
-            pltpu.VMEM((3,) + blocks, BF16),
+            pltpu.VMEM((2,) + halves, BF16),
+            pltpu.VMEM((2,) + halves, BF16),
+            pltpu.VMEM((3,) + halves, BF16),
             pltpu.VMEM((n, 16, tokens), F32),
             pltpu.VMEM((3, tokens, LANES), F32),
             pltpu.VMEM((3,) + blocks, F32),
             pltpu.VMEM((3,) + blocks, F32),
             pltpu.VMEM((3,) + blocks, F32),
-            pltpu.VMEM((2, local, tokens), BF16),
-            pltpu.VMEM((2, local, tokens), BF16),
-            pltpu.VMEM((local, tokens), BF16),
-            pltpu.VMEM((local, tokens), BF16),
-            pltpu.SemaphoreType.DMA((16,)),
-            pltpu.SemaphoreType.DMA((16,)),
+            pltpu.VMEM((2, 2, rows, local), BF16),
+            pltpu.VMEM((2, 2, rows, local), BF16),
+            pltpu.VMEM((tokens, local), BF16),
+            pltpu.VMEM((2, rows, local), BF16),
+            pltpu.SemaphoreType.DMA((SLOTS,)),
+            pltpu.SemaphoreType.DMA((SLOTS,)),
         ],
         compiler_params=pltpu.CompilerParams(
             collective_id=0, has_side_effects=True, vmem_limit_bytes=60 * 1024 * 1024

time: 148 us -> 128 us (0.86)
  Pallas kernels: 147 us -> 127 us
    pallas_call x1, Pallas kernels: 134 us -> 114 us  [shards(): pl.pallas_call(functools.partial(relay_kernel, n), out_shape=(jax.ShapeDt...]
where the time goes in v3:
time: 128 us
  Pallas kernels  127 us (99%)
    pallas_call x1, Pallas kernels, shards(): pl.pallas_call(functools.partial(relay_kernel, n), out_shape=(jax.ShapeDt...  114 us
    pallas_call x1, Pallas kernels, shards(): pl.pallas_call(update_kernel, grid=(steps,), out_shape=tuple((jax.ShapeDt...  12.3 us

profile of v3, /device:TPU:0, one launch (start us, length us, event | category | flops | bytes accessed | tf_op | source)
XLA Modules:
  0.0 128.0 jit_solution(6796633000590247264)
XLA Ops:
  0.6 114.5 %relay.1 = (bf16[256,4096]{1,0:T(8,128)(2,1)}, bf16[256,2048]{1,0:T(8,128)(2,1)}, bf16[224,256]{1,0:T(8,128)(2,1)}, bf16[224,256]{1,0:T(8,128)(2,1)}, bf16[2,1,224,128]{3,2,1,0:T(8,128)(2,1)}) custom-call(s32[2]{0:T(128)} %live_ref.1, bf16[2,1,224,128]{3,2,1,0:T(8,128)(2,1)} %bitcast.15, bf16[2,224,128]{2,1,0:T(8,128)(2,1)} %bitcast.16, ...), custom_call_target="tpu_custom_call" | custom-call | tf_op jit(solution)/shard_map/relay/pallas_call | solution.py:527
  115.1 0.0 copy-start
  115.1 12.3 %update.1 = (bf16[1,224,4096]{2,1,0:T(8,128)(2,1)}, bf16[1,224,2048]{2,1,0:T(8,128)(2,1)}, bf16[1,224,4096]{2,1,0:T(8,128)(2,1)}, bf16[1,224,2048]{2,1,0:T(8,128...) custom-call(bf16[256,4096]{1,0:T(8,128)(2,1)} %get-tuple-element.19.both_ref, ...), custom_call_target="tpu_custom_call" | custom-call | tf_op jit(solution)/shard_map/update/pallas_call | solution.py:570
  127.4 0.0 copy-done
  127.4 0.6 copy.18
Async XLA Ops:
  115.1 12.3 %copy-start = (bf16[2,1,224,128]{3,2,1,0:T(8,128)(2,1)S(1)}, bf16[2,1,224,128]{3,2,1,0:T(8,128)(2,1)}, u32[]{:S(2)}) copy-start(bf16[2,1,224,128]{3,2,1,0:T(8,128)(2,1)} %get-tuple-element.18) | copy-start | bytes 344068

commit v4 on v3

--- a/solution.py
+++ b/solution.py
@@ -18,9 +18,10 @@
 F32 = jnp.float32
 LANES = 128
 
-PRE_SUM, PRE_ALL, GRAD_SUM, GRAD_ALL, HAND = 0, 2, 4, 8, 12
-STATS, MIR_GAINED, MIR_OUT, MIR_PRE, MIR_GRAD, MIR_RMS = 16, 17, 18, 19, 20, 22
-SLOTS = 23
+PRE_LINE, PRE_PLANE, PRE_SHARE, PRE_CAST = 0, 4, 8, 12
+GRAD_SUM, GRAD_ALL, HAND = 16, 20, 24
+STATS, MIR_GAINED, MIR_OUT, MIR_PRE, MIR_GRAD, MIR_RMS = 28, 29, 30, 31, 32, 34
+SLOTS = 35
 
 
 def dot_nt(left, right):
@@ -48,6 +49,8 @@
     inputs_s,
     pre_send,
     pre_recv,
+    pre_mid,
+    pre_last,
     pre_full,
     grad_send,
     grad_recv,
@@ -133,6 +136,38 @@
     def spread(source, target, slot):
         visit(lambda peer: remote(source(peer), target, slot, {"dp": peer}), False)
 
+    ny = 4 if n == 32 else 1
+    nx = half // ny
+    at_z, at_x, at_y = me // half, lax.rem(me, half) // ny, lax.rem(me, ny)
+    lines, planes = (nx, ny), (2 * ny, 2 * nx)
+    on_line = (at_x, at_y)
+    in_plane = (at_z * ny + at_y, at_z * nx + at_x)
+
+    def place(part, th, fb):
+        if part == 0:
+            return (fb // ny) * planes[0] + th * ny + fb % ny
+        return (fb % ny) * planes[1] + th * nx + fb // ny
+
+    def line_block(part, at):
+        return pl.ds(at * planes[part], planes[part])
+
+    def along_line(part, send):
+        for step in (2, 1, 3):
+            if step < lines[part]:
+                at = lax.rem(on_line[part] + step, lines[part])
+                base = at_z * half
+                send(at, base + at * ny + at_y if part == 0 else base + at_x * ny + at)
+
+    def over_plane(part, send):
+        across_z = planes[part] // 2
+        mine = at_y if part == 0 else at_x
+        for dz in (1, 0):
+            for step in (2, 1, 3, 0):
+                if step < across_z and (dz or step):
+                    z, w = lax.rem(at_z + dz, 2), lax.rem(mine + step, across_z)
+                    peer = z * half + (at_x * ny + w if part == 0 else w * ny + at_y)
+                    send(z * across_z + w, peer)
+
     def gain_row(k):
         gains_f = gain_ref[...].astype(F32)
         return jnp.where(section[k] == 0, gains_f[0:1, :], gains_f[1:2, :])
@@ -161,29 +196,77 @@
                 ).astype(BF16)
                 for q in range(2):
                     for th in range(2):
-                        pre_send[k, th * half + 2 * c + q, part] = sums[
+                        pre_send[k, part, place(part, th, 2 * c + q)] = sums[
                             th * rows : (th + 1) * rows, q * LANES : (q + 1) * LANES
                         ]
             return carry
 
         lax.fori_loop(0, chunks, chunk, 0)
-        pre_recv[k, me] = pre_send[k, me]
-
-    def pre_scatter(k):
-        spread(lambda peer: pre_send.at[k, peer], pre_recv.at[k, me], PRE_SUM + k)
-
-    def pre_reduce(k):
-        await_bytes(pre_recv.at[k, pl.ds(0, n - 1)], recv_sems.at[PRE_SUM + k])
         for part in range(2):
-            total = lax.fori_loop(
-                0,
-                n,
-                lambda j, acc: acc + pre_recv[k, j, part].astype(F32),
-                jnp.zeros((rows, LANES), F32),
-                unroll=4,
-            )
-            pre_full[k, me, part] = total.astype(BF16)
-        spread(lambda peer: pre_full.at[k, me], pre_full.at[k, me], PRE_ALL + k)
+            block = line_block(part, on_line[part])
+            pre_recv[k, part, block] = pre_send[k, part, block]
+
+    def pre_line(k):
+        for part in range(2):
+            slot = PRE_LINE + 2 * k + part
+            target = pre_recv.at[k, part, line_block(part, on_line[part])]
+
+            def send(at, peer):
+                remote(pre_send.at[k, part, line_block(part, at)], target, slot, {"dp": peer})
+
+            along_line(part, send)
+
+    def await_some(buffer, k, part, count, slot, sems):
+        if count:
+            await_bytes(buffer.at[k, part, pl.ds(0, count)], sems.at[slot + 2 * k + part])
+
+    def pre_plane(k):
+        for part in range(2):
+            line, plane = lines[part], planes[part]
+            await_some(pre_recv, k, part, (line - 1) * plane, PRE_LINE, recv_sems)
+
+            def block(i, carry):
+                total = pre_recv[k, part, i].astype(F32)
+                for at in range(1, line):
+                    total += pre_recv[k, part, at * plane + i].astype(F32)
+                pre_mid[k, part, i] = total.astype(BF16)
+                return carry
+
+            lax.fori_loop(0, plane, block, 0)
+            mine = in_plane[part]
+            pre_last[k, part, mine] = pre_mid[k, part, mine]
+
+            def send(at, peer):
+                slot = PRE_PLANE + 2 * k + part
+                remote(pre_mid.at[k, part, at], pre_last.at[k, part, mine], slot, {"dp": peer})
+
+            over_plane(part, send)
+
+    def pre_share(k):
+        for part in range(2):
+            plane = planes[part]
+            await_some(pre_last, k, part, plane - 1, PRE_PLANE, recv_sems)
+            total = pre_last[k, part, 0].astype(F32)
+            for i in range(1, plane):
+                total += pre_last[k, part, i].astype(F32)
+            here = on_line[part] * plane + in_plane[part]
+            pre_full[k, part, here] = total.astype(BF16)
+            mine = pre_full.at[k, part, here]
+
+            def send(at, peer):
+                remote(mine, mine, PRE_SHARE + 2 * k + part, {"dp": peer})
+
+            over_plane(part, send)
+
+    def pre_cast(k):
+        for part in range(2):
+            await_some(pre_full, k, part, planes[part] - 1, PRE_SHARE, recv_sems)
+            mine = pre_full.at[k, part, line_block(part, on_line[part])]
+
+            def send(at, peer):
+                remote(mine, mine, PRE_CAST + 2 * k + part, {"dp": peer})
+
+            along_line(part, send)
 
     def coefficients(k, row_at):
         for th in range(2):
@@ -191,8 +274,8 @@
 
             def block(fb, carry):
                 j = th * half + fb
-                gate_pre = pre_full[k, j, 0].astype(F32)
-                up_pre = pre_full[k, j, 1].astype(F32)
+                gate_pre = pre_full[k, 0, place(0, th, fb)].astype(F32)
+                up_pre = pre_full[k, 1, place(1, th, fb)].astype(F32)
                 gate_val = scale * gate_pre
                 up_val = scale * up_pre
                 sigma = jax.nn.sigmoid(gate_val)
@@ -210,7 +293,9 @@
             lax.fori_loop(0, half, block, 0, unroll=2)
 
     def pre_finish(k):
-        await_bytes(pre_full.at[k, pl.ds(0, n - 1)], recv_sems.at[PRE_ALL + k])
+        for part in range(2):
+            count = (lines[part] - 1) * planes[part]
+            await_some(pre_full, k, part, count, PRE_CAST, recv_sems)
         coefficients(k, pl.multiple_of(section[k] * tokens, tokens))
 
         @pl.when(section[k] == 1)
@@ -346,40 +431,50 @@
 
     @for_outer
     def _():
-        pre_scatter(0)
+        pre_line(0)
         grad_scatter(0, 0)
         grad_scatter(0, 1)
 
-    pre_partial(1)
-    rms_finish()
-
     @for_inner
     def _():
-        pre_scatter(0)
+        pre_partial(1)
+        rms_finish()
+        pre_line(0)
+
+    pre_plane(0)
+
+    @for_outer
+    def _():
+        pre_partial(1)
+        rms_finish()
 
     remote(gained_s.at[high], gained_mir, MIR_GAINED, {"pipe": 3 - pipe})
-    pre_reduce(0)
+
+    pre_share(0)
 
     @for_outer
     def _():
         grad_reduce(0, 0)
         grad_reduce(0, 1)
 
+    pre_cast(0)
+    pre_finish(0)
+
     @for_inner
     def _():
-        pre_scatter(1)
-
-    pre_finish(0)
+        pre_line(1)
 
     @for_outer
     def _():
         for h in range(2):
             grad_finish(0, h)
             remote(next_s.at[0, h], hand.at[0, h], HAND + h, {"pipe": pipe + 1 - 2 * high})
-        pre_scatter(1)
+        pre_line(1)
         mirror_grads(0)
         gin_ref[section[0], 0] = flipped(next_s[0])
-        pre_reduce(1)
+        pre_plane(1)
+        pre_share(1)
+        pre_cast(1)
         pre_finish(1)
 
     @for_inner
@@ -387,12 +482,14 @@
         for h in range(2):
             await_bytes(hand.at[0, h], recv_sems.at[HAND + h])
             grad_scatter(0, h)
+        pre_plane(1)
         grad_reduce(0, 0)
         grad_reduce(0, 1)
-        pre_reduce(1)
+        pre_share(1)
         for h in range(2):
             grad_finish(0, h)
             remote(next_s.at[0, h], hand.at[1, h], HAND + 2 + h, {"pipe": pipe + 1 - 2 * high})
+        pre_cast(1)
         mirror_grads(0)
         gin_ref[section[0], 0] = flipped(next_s[0])
 
@@ -439,8 +536,12 @@
     gout_ref[:, pl.ds(tokens, tokens)] = flipped(out_mir[...])
 
     for k in range(2):
-        await_bytes(pre_send.at[k, pl.ds(0, n - 1)], send_sems.at[PRE_SUM + k])
-        await_bytes(pre_full.at[k, pl.ds(0, n - 1)], send_sems.at[PRE_ALL + k])
+        for part in range(2):
+            line, plane = lines[part], planes[part]
+            await_some(pre_send, k, part, (line - 1) * plane, PRE_LINE, send_sems)
+            await_some(pre_mid, k, part, plane - 1, PRE_PLANE, send_sems)
+            await_some(pre_full, k, part, plane - 1, PRE_SHARE, send_sems)
+            await_some(pre_full, k, part, (line - 1) * plane, PRE_CAST, send_sems)
         for h in range(2):
             spans = pl.ds(0, n - 1)
             await_bytes(grad_send.at[k, h, spans], send_sems.at[GRAD_SUM + 2 * k + h])
@@ -538,9 +639,11 @@
         scratch_shapes=[
             pltpu.VMEM((2, tokens, local), BF16),
             pltpu.VMEM((2, tokens, local), F32),
-            pltpu.VMEM((2, n, 2, rows, LANES), BF16),
-            pltpu.VMEM((2, n, 2, rows, LANES), BF16),
-            pltpu.VMEM((3, n, 2, rows, LANES), BF16),
+            pltpu.VMEM((2, 2) + blocks, BF16),
+            pltpu.VMEM((2, 2) + blocks, BF16),
+            pltpu.VMEM((2, 2, 8, rows, LANES), BF16),
+            pltpu.VMEM((2, 2, 8, rows, LANES), BF16),
+            pltpu.VMEM((3, 2) + blocks, BF16),
             pltpu.VMEM((2,) + halves, BF16),
             pltpu.VMEM((2,) + halves, BF16),
             pltpu.VMEM((3,) + halves, BF16),
@@ -562,7 +665,7 @@
         name="relay",
     )(live_tokens, x_t, loss_t, jnp.reshape(gains, (2, local)), w_in, wout_t)
 
-    steps = 8
+    steps = 4
     wide, tall = 2 * hidden // steps, hidden // steps
     in_block = pl.BlockSpec((1, local, wide), lambda i: (0, 0, i))
     out_block = pl.BlockSpec((1, local, tall), lambda i: (0, 0, i))

time: 128 us -> 117 us (0.914)
  the two profiles are of different devices: /device:TPU:0 before, /device:TPU:1 now
where the time goes in v4:
time: 117 us
  Pallas kernels  115 us (98%)
    pallas_call x1, Pallas kernels, shards(): pl.pallas_call(functools.partial(relay_kernel, n), out_shape=(jax.ShapeDt...  105 us
    pallas_call x1, Pallas kernels, shards(): pl.pallas_call(update_kernel, grid=(steps,), out_shape=tuple((jax.ShapeDt...  10.4 us

profile of v4, /device:TPU:1, one launch (start us, length us, event | category | flops | bytes accessed | tf_op | source)
XLA Modules:
  0.0 116.6 jit_solution(2023975275286501699)
XLA Ops:
  0.6 104.9 %relay.1 = (bf16[256,4096]{1,0:T(8,128)(2,1)}, bf16[256,2048]{1,0:T(8,128)(2,1)}, bf16[224,256]{1,0:T(8,128)(2,1)}, bf16[224,256]{1,0:T(8,128)(2,1)}, bf16[2,1,224,128]{3,2,1,0:T(8,128)(2,1)}) custom-call(s32[2]{0:T(128)} %live_ref.1, bf16[2,1,224,128]{3,2,1,0:T(8,128)(2,1)} %bitcast.15, bf16[2,224,128]{2,1,0:T(8,128)(2,1)} %bitcast.16, ...), custom_call_target="tpu_custom_call" | custom-call | tf_op jit(solution)/shard_map/relay/pallas_call | solution.py:628
  105.5 0.0 copy-start
  105.5 10.4 %update.1 = (bf16[1,224,4096]{2,1,0:T(8,128)(2,1)}, bf16[1,224,2048]{2,1,0:T(8,128)(2,1)}, bf16[1,224,4096]{2,1,0:T(8,128)(2,1)}, bf16[1,224,2048]{2,1,0:T(8,128...) custom-call(bf16[256,4096]{1,0:T(8,128)(2,1)} %get-tuple-element.19.both_ref, ...), custom_call_target="tpu_custom_call" | custom-call | tf_op jit(solution)/shard_map/update/pallas_call | solution.py:673
  115.9 0.0 copy-done
  115.9 0.6 copy.18
Async XLA Ops:
  105.5 10.4 %copy-start = (bf16[2,1,224,128]{3,2,1,0:T(8,128)(2,1)S(1)}, bf16[2,1,224,128]{3,2,1,0:T(8,128)(2,1)}, u32[]{:S(2)}) copy-start(bf16[2,1,224,128]{3,2,1,0:T(8,128)(2,1)} %get-tuple-element.18) | copy-start | bytes 344068
